TPU v7x, 32 devices: a whole 2x2x4 slice. The times are simulated.
32 devices in a mesh: dp: 16 (over z, y, x), fsdp: 2 (over core).
Axes of the slice: x: 2, y: 2, z: 4, core: 2. Of those that a mesh axis runs over, the one named last changes fastest.
Arguments:
- hidden_in: bfloat16 [32, 1024, 768], P(('dp', 'fsdp')), may hold values from -6 to 6
- row_grad: bfloat16 [32, 1024, 768], P(('dp', 'fsdp')), may hold values from -6 to 6
- segment_ids: int32 [32, 1024], P(('dp', 'fsdp')), may hold values from 0 to 15, as said below
- query_cls: int32 [32, 8], P(('dp', 'fsdp')), may hold values from 0 to 1022, as said below
- passage_cls: int32 [32, 8], P(('dp', 'fsdp')), may hold values from 16 to 1023, as said below
- positives: int32 [256], replicated, may hold values from 0 to 255
- w_query: float32 [768, 768], P(('dp', 'fsdp')), may hold values from -0.3125 to 0.3125
- w_key: float32 [768, 768], P(('dp', 'fsdp')), may hold values from -0.21875 to 0.21875
- w_value: float32 [768, 768], P(('dp', 'fsdp')), may hold values from -0.21875 to 0.21875
- w_output: float32 [768, 768], P(('dp', 'fsdp')), may hold values from -0.625 to 0.625
- b_query: float32 [768], P(('dp', 'fsdp')), may hold values from -3 to 3
- b_value: float32 [768], P(('dp', 'fsdp')), may hold values from -3 to 3
- b_output: float32 [768], P(('dp', 'fsdp')), may hold values from -3 to 3
- attn_gain: float32 [768], P(('dp', 'fsdp')), may hold values from 0.5 to 1.5
- attn_shift: float32 [768], P(('dp', 'fsdp')), may hold values from -2 to 2
- w_inner: float32 [768, 3072], P(('dp', 'fsdp')), may hold values from -0.21875 to 0.21875
- b_inner: float32 [3072], P(('dp', 'fsdp')), may hold values from -3 to 3
- w_outer: float32 [3072, 768], P(('dp', 'fsdp')), may hold values from -0.109375 to 0.109375
- b_outer: float32 [768], P(('dp', 'fsdp')), may hold values from -2 to 2
- ffn_gain: float32 [768], P(('dp', 'fsdp')), may hold values from 0.5 to 1.5
- ffn_shift: float32 [768], P(('dp', 'fsdp')), may hold values from -2 to 2
Outputs:
- query_loss: float32 [256], P(('dp', 'fsdp'))
- hidden_out: bfloat16 [32, 1024, 768], P(('dp', 'fsdp'))
- hidden_grad: float32 [32, 1024, 768], P(('dp', 'fsdp'))
- w_query_grad: float32 [768, 768], P(('dp', 'fsdp'))
- w_key_grad: float32 [768, 768], P(('dp', 'fsdp'))
- w_value_grad: float32 [768, 768], P(('dp', 'fsdp'))
- w_output_grad: float32 [768, 768], P(('dp', 'fsdp'))
- b_query_grad: float32 [768], P(('dp', 'fsdp'))
- b_value_grad: float32 [768], P(('dp', 'fsdp'))
- b_output_grad: float32 [768], P(('dp', 'fsdp'))
- attn_gain_grad: float32 [768], P(('dp', 'fsdp'))
- attn_shift_grad: float32 [768], P(('dp', 'fsdp'))
- w_inner_grad: float32 [768, 3072], P(('dp', 'fsdp'))
- b_inner_grad: float32 [3072], P(('dp', 'fsdp'))
- w_outer_grad: float32 [3072, 768], P(('dp', 'fsdp'))
- b_outer_grad: float32 [768], P(('dp', 'fsdp'))
- ffn_gain_grad: float32 [768], P(('dp', 'fsdp'))
- ffn_shift_grad: float32 [768], P(('dp', 'fsdp'))
Inputs may be any that keep to these rules, and one draw needn't show every extreme that they name: `segment_ids`: each row holds 16 segments numbered in order of position, a query segment (even number) and a passage segment (odd number) alternating. `query_cls`: the first position of each query segment of the row, in order. `passage_cls`: the first position of each passage segment of the row, in order.
All inputs are finite; a program needn't handle non-finite values.
Results may differ from a plain program's by a relative error of at most 0.013.
The roundings to bfloat16 on the way count: a program that leaves them out, or rounds other values in their place, can miss the bound.
Values may be sent and summed in bfloat16 or wider, within the bound.
No kernel may reach another device: no remote copies, remote signals or barrier semaphores. Data moves between devices by JAX's collectives and lax.ppermute only.
A program may use at most 256 MiB of HBM per device.

v0:
```python
import math

import jax
import jax.numpy as jnp
from jax import lax
from jax.sharding import PartitionSpec as P

HEADS = 12
HEAD = 64


EPS = 1e-12
NEG = -1e30


def matmul(left, right):
    return jnp.dot(left, right, preferred_element_type=jnp.float32)


def contract_rows(left, right):
    return lax.dot_general(
        left, right, (((0,), (0,)), ((), ())), preferred_element_type=jnp.float32
    )


def contract_cols(left, right):
    return lax.dot_general(
        left, right, (((1,), (1,)), ((), ())), preferred_element_type=jnp.float32
    )


def heads_view(block):
    return block.reshape(block.shape[0], HEADS, HEAD)


def norm_forward(value, gain, shift):
    mean = jnp.mean(value, axis=-1, keepdims=True)
    centred = value - mean
    spread = jnp.mean(centred * centred, axis=-1, keepdims=True)
    scaling = lax.rsqrt(spread + EPS)
    normed = centred * scaling
    return (normed * gain + shift, normed, scaling)


def norm_backward(grad, normed, scaling, gain):
    scaled = grad * gain
    first_mean = jnp.mean(scaled, axis=-1, keepdims=True)
    second_mean = jnp.mean(scaled * normed, axis=-1, keepdims=True)
    result = scaling * (scaled - first_mean - normed * second_mean)
    return (result, jnp.sum(grad * normed, axis=0), jnp.sum(grad, axis=0))


def gelu_parts(pre_act):
    cdf_part = 0.5 * (1.0 + lax.erf(pre_act * (1.0 / math.sqrt(2.0))))
    slope = cdf_part + pre_act * jnp.exp(-0.5 * pre_act * pre_act) * (
        1.0 / math.sqrt(2.0 * math.pi)
    )
    return (pre_act * cdf_part, slope)


def block_scores(query_block, key_row, query_segment, key_segment):
    raw_scores = jnp.einsum(
        "qhd,khd->hqk",
        heads_view(query_block),
        heads_view(key_row),
        preferred_element_type=jnp.float32,
    )
    same = query_segment[:, None] == key_segment[None, :]
    return jnp.where(same[None], raw_scores * HEAD ** (-0.5), NEG)


def body(
    hidden_in,
    row_grad,
    segment_ids,
    query_cls,
    passage_cls,
    positives,
    w_query,
    w_key,
    w_value,
    w_output,
    b_query,
    b_value,
    b_output,
    attn_gain,
    attn_shift,
    w_inner,
    b_inner,
    w_outer,
    b_outer,
    ffn_gain,
    ffn_shift,
):
    rows, length, width = hidden_in.shape
    tokens = rows * length
    span = min(512, length)
    per_row = length // span
    inputs = hidden_in.reshape(tokens, width)
    residual_in = inputs.astype(jnp.float32)
    segment_flat = segment_ids.reshape(tokens)
    attn_params = (
        lax.all_gather(w_query.astype(jnp.bfloat16), ("dp", "fsdp"), axis=0, tiled=True),
        lax.all_gather(w_key.astype(jnp.bfloat16), ("dp", "fsdp"), axis=0, tiled=True),
        lax.all_gather(w_value.astype(jnp.bfloat16), ("dp", "fsdp"), axis=0, tiled=True),
        lax.all_gather(w_output.astype(jnp.bfloat16), ("dp", "fsdp"), axis=0, tiled=True),
        lax.all_gather(b_query.astype(jnp.bfloat16), ("dp", "fsdp"), axis=0, tiled=True),
        lax.all_gather(b_value.astype(jnp.bfloat16), ("dp", "fsdp"), axis=0, tiled=True),
        lax.all_gather(b_output.astype(jnp.bfloat16), ("dp", "fsdp"), axis=0, tiled=True),
        lax.all_gather(attn_gain.astype(jnp.bfloat16), ("dp", "fsdp"), axis=0, tiled=True),
        lax.all_gather(attn_shift.astype(jnp.bfloat16), ("dp", "fsdp"), axis=0, tiled=True),
    )
    (
        query_mat,
        key_mat,
        value_mat,
        output_mat,
        query_bias,
        value_bias,
        output_bias,
        gain_one,
        shift_one,
    ) = attn_params
    gain_one = gain_one.astype(jnp.float32)
    queries = (matmul(inputs, query_mat) + query_bias.astype(jnp.float32)).astype(jnp.bfloat16)
    keys_all = matmul(inputs, key_mat).astype(jnp.bfloat16)
    values = (matmul(inputs, value_mat) + value_bias.astype(jnp.float32)).astype(jnp.bfloat16)

    def block_parts(index):
        query_start = index * span
        return (
            lax.dynamic_slice_in_dim(queries, query_start, span, 0),
            keys_all,
            values,
            lax.dynamic_slice_in_dim(segment_flat, query_start, span, 0),
            segment_flat,
            query_start,
        )

    def attend(index):
        query_block, key_row, value_row, query_segment, key_segment, query_start = block_parts(
            index
        )
        scores = block_scores(query_block, key_row, query_segment, key_segment)
        highest = jnp.max(scores, axis=-1, keepdims=True)
        exp_scores = jnp.exp(scores - highest)
        total = jnp.sum(exp_scores, axis=-1, keepdims=True)
        probs = (exp_scores / total).astype(jnp.bfloat16)
        context = jnp.einsum(
            "hqk,khd->qhd", probs, heads_view(value_row), preferred_element_type=jnp.float32
        )
        return (
            context.reshape(span, width).astype(jnp.bfloat16),
            (highest + jnp.log(total))[..., 0],
        )

    block_ids = jnp.arange(rows * per_row, dtype=jnp.int32)
    context_blocks, log_totals = lax.map(attend, block_ids)
    context = context_blocks.reshape(tokens, width)
    branch = matmul(context, output_mat) + output_bias.astype(jnp.float32)
    middle, normed_one, scaling_one = norm_forward(
        residual_in + branch, gain_one, shift_one.astype(jnp.float32)
    )
    middle_low = middle.astype(jnp.bfloat16)
    ffn_params = (
        lax.all_gather(w_inner.astype(jnp.bfloat16), ("dp", "fsdp"), axis=0, tiled=True),
        lax.all_gather(w_outer.astype(jnp.bfloat16), ("dp", "fsdp"), axis=0, tiled=True),
        lax.all_gather(b_inner.astype(jnp.bfloat16), ("dp", "fsdp"), axis=0, tiled=True),
        lax.all_gather(b_outer.astype(jnp.bfloat16), ("dp", "fsdp"), axis=0, tiled=True),
        lax.all_gather(ffn_gain.astype(jnp.bfloat16), ("dp", "fsdp"), axis=0, tiled=True),
        lax.all_gather(ffn_shift.astype(jnp.bfloat16), ("dp", "fsdp"), axis=0, tiled=True),
    )
    inner_mat, outer_mat, inner_bias, outer_bias, gain_two, shift_two = ffn_params
    gain_two = gain_two.astype(jnp.float32)
    pre_act = matmul(middle_low, inner_mat) + inner_bias.astype(jnp.float32)
    activated, slope = gelu_parts(pre_act)
    act_low = activated.astype(jnp.bfloat16)
    update = matmul(act_low, outer_mat) + outer_bias.astype(jnp.float32)
    output, normed_two, scaling_two = norm_forward(
        middle + update, gain_two, shift_two.astype(jnp.float32)
    )
    pairs = query_cls.shape[1]
    count = rows * pairs
    row_base = (jnp.arange(rows, dtype=jnp.int32) * length)[:, None]
    query_index = (query_cls + row_base).reshape(count)
    passage_index = (passage_cls + row_base).reshape(count)
    query_emb = output[query_index].astype(jnp.bfloat16)
    passage_emb = output[passage_index].astype(jnp.bfloat16)
    score_scale = 4.0 / math.sqrt(width)
    all_passages = lax.all_gather(passage_emb, ("dp", "fsdp"), axis=0, tiled=True)
    columns = all_passages.shape[0]
    first = lax.axis_index(("dp", "fsdp")) * count
    scores = contract_cols(query_emb, all_passages) * score_scale
    own_positives = lax.dynamic_slice_in_dim(positives, first, count, 0)
    column_ids = jnp.arange(columns, dtype=jnp.int32)
    hit = (column_ids[None, :] == own_positives[:, None]).astype(jnp.float32)
    highest = jnp.max(scores, axis=-1, keepdims=True)
    log_total = highest[:, 0] + jnp.log(jnp.sum(jnp.exp(scores - highest), axis=-1))
    query_loss = log_total - jnp.sum(hit * scores, axis=-1)
    score_grad = ((jnp.exp(scores - log_total[:, None]) - hit) * score_scale).astype(jnp.bfloat16)
    query_emb_grad = matmul(score_grad, all_passages)
    passage_emb_grad = lax.psum_scatter(
        contract_rows(score_grad, query_emb), ("dp", "fsdp"), scatter_dimension=0, tiled=True
    )
    out_grad = row_grad.reshape(tokens, width).astype(jnp.float32)
    out_grad = out_grad.at[query_index].add(query_emb_grad).at[passage_index].add(passage_emb_grad)
    sum_grad, gain_two_grad, shift_two_grad = norm_backward(
        out_grad, normed_two, scaling_two, gain_two
    )
    update_grad = sum_grad.astype(jnp.bfloat16)
    outer_grad = contract_rows(act_low, update_grad)
    outer_bias_grad = jnp.sum(update_grad.astype(jnp.float32), axis=0)
    pre_grad = (contract_cols(update_grad, outer_mat) * slope).astype(jnp.bfloat16)
    inner_grad = contract_rows(middle_low, pre_grad)
    inner_bias_grad = jnp.sum(pre_grad.astype(jnp.float32), axis=0)
    middle_grad = sum_grad + contract_cols(pre_grad, inner_mat)
    ffn_grads = (
        lax.psum_scatter(inner_grad, ("dp", "fsdp"), scatter_dimension=0, tiled=True),
        lax.psum_scatter(inner_bias_grad, ("dp", "fsdp"), scatter_dimension=0, tiled=True),
        lax.psum_scatter(outer_grad, ("dp", "fsdp"), scatter_dimension=0, tiled=True),
        lax.psum_scatter(outer_bias_grad, ("dp", "fsdp"), scatter_dimension=0, tiled=True),
        lax.psum_scatter(gain_two_grad, ("dp", "fsdp"), scatter_dimension=0, tiled=True),
        lax.psum_scatter(shift_two_grad, ("dp", "fsdp"), scatter_dimension=0, tiled=True),
    )
    first_grad, gain_one_grad, shift_one_grad = norm_backward(
        middle_grad, normed_one, scaling_one, gain_one
    )
    branch_grad = first_grad.astype(jnp.bfloat16)
    output_w_grad = contract_rows(context, branch_grad)
    output_bias_grad = jnp.sum(branch_grad.astype(jnp.float32), axis=0)
    context_grad = contract_cols(branch_grad, output_mat).astype(jnp.bfloat16)

    def attend_back(item):
        index, log_block = item
        query_block, key_row, value_row, query_segment, key_segment, query_start = block_parts(
            index
        )
        context_block = lax.dynamic_slice_in_dim(context_grad, query_start, span, 0)
        scores_again = block_scores(query_block, key_row, query_segment, key_segment)
        probs = jnp.exp(scores_again - log_block[..., None])
        prob_grad = jnp.einsum(
            "qhd,khd->hqk",
            heads_view(context_block),
            heads_view(value_row),
            preferred_element_type=jnp.float32,
        )
        value_part = jnp.einsum(
            "hqk,qhd->khd",
            probs.astype(jnp.bfloat16),
            heads_view(context_block),
            preferred_element_type=jnp.float32,
        )
        inner_sum = jnp.sum(probs * prob_grad, axis=-1, keepdims=True)
        score_part = (probs * (prob_grad - inner_sum)).astype(jnp.bfloat16)
        query_part = jnp.einsum(
            "hqk,khd->qhd", score_part, heads_view(key_row), preferred_element_type=jnp.float32
        ) * HEAD ** (-0.5)
        key_part = jnp.einsum(
            "hqk,qhd->khd", score_part, heads_view(query_block), preferred_element_type=jnp.float32
        ) * HEAD ** (-0.5)
        return (
            query_part.reshape(span, width),
            key_part.reshape(length, width),
            value_part.reshape(length, width),
        )

    query_parts, key_parts, value_parts = lax.map(attend_back, (block_ids, log_totals))
    query_grad = query_parts.reshape(tokens, width).astype(jnp.bfloat16)
    key_grad = (
        key_parts.reshape(rows, per_row, length, width)
        .sum(axis=1)
        .reshape(tokens, width)
        .astype(jnp.bfloat16)
    )
    value_grad = (
        value_parts.reshape(rows, per_row, length, width)
        .sum(axis=1)
        .reshape(tokens, width)
        .astype(jnp.bfloat16)
    )
    query_w_grad = contract_rows(inputs, query_grad)
    key_w_grad = contract_rows(inputs, key_grad)
    value_w_grad = contract_rows(inputs, value_grad)
    query_bias_grad = jnp.sum(query_grad.astype(jnp.float32), axis=0)
    value_bias_grad = jnp.sum(value_grad.astype(jnp.float32), axis=0)
    hidden_grad = (
        first_grad
        + contract_cols(query_grad, query_mat)
        + contract_cols(key_grad, key_mat)
        + contract_cols(value_grad, value_mat)
    )
    attn_grads = (
        lax.psum_scatter(query_w_grad, ("dp", "fsdp"), scatter_dimension=0, tiled=True),
        lax.psum_scatter(key_w_grad, ("dp", "fsdp"), scatter_dimension=0, tiled=True),
        lax.psum_scatter(value_w_grad, ("dp", "fsdp"), scatter_dimension=0, tiled=True),
        lax.psum_scatter(output_w_grad, ("dp", "fsdp"), scatter_dimension=0, tiled=True),
        lax.psum_scatter(query_bias_grad, ("dp", "fsdp"), scatter_dimension=0, tiled=True),
        lax.psum_scatter(value_bias_grad, ("dp", "fsdp"), scatter_dimension=0, tiled=True),
        lax.psum_scatter(output_bias_grad, ("dp", "fsdp"), scatter_dimension=0, tiled=True),
        lax.psum_scatter(gain_one_grad, ("dp", "fsdp"), scatter_dimension=0, tiled=True),
        lax.psum_scatter(shift_one_grad, ("dp", "fsdp"), scatter_dimension=0, tiled=True),
    )
    hidden_out = output.reshape(rows, length, width).astype(jnp.bfloat16)
    return (
        (query_loss, hidden_out, hidden_grad.reshape(rows, length, width))
        + tuple(attn_grads)
        + tuple(ffn_grads)
    )


def solution(mesh):
    placed = (
        P(("dp", "fsdp"), None, None),
        P(("dp", "fsdp"), None, None),
        P(("dp", "fsdp"), None),
        P(("dp", "fsdp"), None),
        P(("dp", "fsdp"), None),
        P(),
        P(("dp", "fsdp"), None),
        P(("dp", "fsdp"), None),
        P(("dp", "fsdp"), None),
        P(("dp", "fsdp"), None),
        P(("dp", "fsdp")),
        P(("dp", "fsdp")),
        P(("dp", "fsdp")),
        P(("dp", "fsdp")),
        P(("dp", "fsdp")),
        P(("dp", "fsdp"), None),
        P(("dp", "fsdp")),
        P(("dp", "fsdp"), None),
        P(("dp", "fsdp")),
        P(("dp", "fsdp")),
        P(("dp", "fsdp")),
    )
    return jax.shard_map(
        body,
        mesh=mesh,
        in_specs=placed,
        out_specs=(
            P(("dp", "fsdp")),
            P(("dp", "fsdp"), None, None),
            P(("dp", "fsdp"), None, None),
            P(("dp", "fsdp"), None),
            P(("dp", "fsdp"), None),
            P(("dp", "fsdp"), None),
            P(("dp", "fsdp"), None),
            P(("dp", "fsdp")),
            P(("dp", "fsdp")),
            P(("dp", "fsdp")),
            P(("dp", "fsdp")),
            P(("dp", "fsdp")),
            P(("dp", "fsdp"), None),
            P(("dp", "fsdp")),
            P(("dp", "fsdp"), None),
            P(("dp", "fsdp")),
            P(("dp", "fsdp")),
            P(("dp", "fsdp")),
        ),
        check_vma=False,
    )
```

profile of v0, /device:TPU:0, one launch (start us, length us, event | category | flops | bytes accessed | tf_op | source)
XLA Modules:
  0.0 1375.8 jit_solution(13707741930182174458)
XLA Ops:
  27.5 42.6 %all-reduce.19 = (bf16[768]{0:T(1024)(128)(2,1)S(1)}, bf16[768]{0:T(1024)(128)(2,1)S(1)}, bf16[768]{0:T(1024)(128)(2,1)S(1)}, bf16[768]{0:T(1024)(128)(2,1)S(1)}...) all-reduce(bf16[768]{0:T(1024)(128)(2,1)S(1)} %dynamic-update-slice, ...), channel_id=1, replica_groups=mesh['dp'=16,'fsdp'=2] {'dp','fsdp'}, use_global_device_ids=true, to_apply=%add | all-reduce | flops 9216 | bytes 36864
  81.8 42.8 %all-gather.7.cloned.1.call-done = bf16[768,768]{1,0:T(8,128)(2,1)} async-done(((bf16[24,768]{1,0:T(8,128)(2,1)}), bf16[768,768]{1,0:T(8,128)(2,1)}) %all-gather.7.cloned.1.call-update) | async-done | bytes 1179664 | tf_op jit(solution)/shard_map/all_gather | solution.py:103
  130.2 50.8 %all-gather.9.cloned.1.call-done = bf16[768,768]{1,0:T(8,128)(2,1)} async-done(((bf16[24,768]{1,0:T(8,128)(2,1)}), bf16[768,768]{1,0:T(8,128)(2,1)}) %all-gather.9.cloned.1.call-update) | async-done | bytes 1179664 | tf_op jit(solution)/shard_map/all_gather | solution.py:104
  187.9 79.6 %while.26 = (s32[]{:T(128)}, bf16[2,512,768]{2,1,0:T(8,128)(2,1)}, f32[2,12,512]{2,1,0:T(8,128)S(1)}, s32[2]{0:T(128)S(1)}, s32[1024]{0:T(1024)S(1)}, /*index=5*...) while((s32[]{:T(128)}, bf16[2,512,768]{2,1,0:T(8,128)(2,1)}, ...), condition=%wide.region_3.4_spmd, body=%wide.region_0.3_spmd.sunk | while | flops 1687021568 | bytes 187926768 | solution.py:158
  189.6 12.1 fusion.115
  201.7 12.3 fusion.116
  229.2 12.1 fusion.115
  241.3 12.3 fusion.116
  274.1 29.0 %all-gather.15.cloned.1.call-done = bf16[768,3072]{1,0:T(8,128)(2,1)} async-done(((bf16[24,3072]{1,0:T(8,128)(2,1)}), bf16[768,3072]{1,0:T(8,128)(2,1)}) %all-gather.15.cloned.1.call-update) | async-done | bytes 4718608 | tf_op jit(solution)/shard_map/all_gather | solution.py:166
  303.1 13.6 multiply_convert_fusion.1
  316.7 51.6 %all-gather.17.cloned.1.call-done = bf16[3072,768]{1,0:T(8,128)(2,1)} async-done(((bf16[96,768]{1,0:T(8,128)(2,1)}), bf16[3072,768]{1,0:T(8,128)(2,1)}) %all-gather.17.cloned.1.call-update) | async-done | bytes 4718608 | tf_op jit(solution)/shard_map/all_gather | solution.py:167
  388.6 40.1 %all_gather.63 = bf16[256,768]{1,0:T(8,128)(2,1)S(1)} all-gather(bf16[8,768]{1,0:T(8,128)(2,1)} %gather_fusion.1), channel_id=1, replica_groups=mesh['dp'=16,'fsdp'=2] {'dp','fsdp'}, dimensions={0}, use_global_device_ids=true | all-gather | bytes 405504 | tf_op jit(solution)/shard_map/all_gather | solution.py:190
  442.3 84.0 %reduce-scatter.14.cloned.1.call-done = f32[8,768]{1,0:T(8,128)} async-done(((f32[256,768]{1,0:T(8,128)}), f32[8,768]{1,0:T(8,128)}) %reduce-scatter.14.cloned.1.call-update) | async-done | bytes 24592 | tf_op jit(solution)/shard_map/reduce_scatter | solution.py:202
  539.8 13.8 %convert_reduce_fusion = (f32[3072]{0:T(1024)}, bf16[1024,3072]{1,0:T(8,128)(2,1)S(1)}) fusion(f32[1024,3072]{1,0:T(8,128)} %get-tuple-element.336, f32[3072]{0:T(1024)S(1)} %copy-done.47, bf16[3072,768]{1,0:T(8,128)(2,1)} %all-gather.17.cloned.1.call-done, f32[1024,768]{0,1:T(8,128)S(1)} %get-tuple-element.322), kind=kOutput, calls=%fused_computation.41 | convolution fusion | flops 4873516032 | bytes 26763264 | tf_op jit(solution)/shard_map/dot_general | solution.py:27
  568.8 198.4 %while.27 = (s32[]{:T(128)}, bf16[2,512,768]{2,1,0:T(8,128)(2,1)}, f32[2,1024,768]{1,2,0:T(8,128)}, f32[2,1024,768]{1,2,0:T(8,128)}, s32[2]{0:T(128)S(1)}, /*ind...) while((s32[]{:T(128)}, bf16[2,512,768]{2,1,0:T(8,128)(2,1)}, ...), condition=%wide.region_20.21_spmd, body=%wide.region_18.20_spmd.sunk | while | flops 4122994688 | bytes 229558544 | solution.py:267
  574.5 11.8 fusion.128
  586.3 13.4 fusion.129
  599.7 20.3 %multiply_reduce_fusion.10 = (f32[12,512]{1,0:T(8,128)S(1)}, f32[12,512,1024]{2,1,0:T(8,128)}) fusion(f32[12,512,1024]{2,1,0:T(8,128)} %fusion.128, f32[12,512]{1,0:T(8,128)S(1)} %dynamic-slice_bitcast_fusion.2, pred[512,1024]{1,0:T(8,128)(4,1)S(1)} %broadcast_compare_fusion.5, bf16[512,12,64]{0,2,1:T(8,128)(2,1)S(1)} %bitcast.180, ...), kind=kOutput, calls=%fused_computation.18.clone.1 | convolution fusion | flops 836757504 | bytes 53264384 | tf_op jit(solution)/shard_map/while/body/eval_jaxpr/qhd,khd->hqk/dot_general | solution.py:241
  620.1 22.1 %multiply_convert_fusion.6 = bf16[12,512,1024]{2,1,0:T(8,128)(2,1)} fusion(f32[12,512,1024]{2,1,0:T(8,128)} %get-tuple-element.482, f32[12,512,1024]{2,1,0:T(8,128)} %fusion.128, f32[12,512]{1,0:T(8,128)S(1)} %get-tuple-element.483, f32[12,512]{1,0:T(8,128)S(1)} %dynamic-slice_bitcast_fusion.2, pred[512,1024]{1,0:T(8,128)(4,1)S(1)} %broadcast_compare_fusion.5), kind=kLoop, calls=%fused_computation.17.clone.1 | loop fusion | flops 37748736 | bytes 63488000 | tf_op jit(solution)/shard_map/while/body/eval_jaxpr/convert_element_type | solution.py:254
  642.2 9.9 convolution_multiply_fusion.5
  674.1 11.6 fusion.128
  685.7 13.1 fusion.129
  698.8 20.2 %multiply_reduce_fusion.10 = (f32[12,512]{1,0:T(8,128)S(1)}, f32[12,512,1024]{2,1,0:T(8,128)}) fusion(f32[12,512,1024]{2,1,0:T(8,128)} %fusion.128, f32[12,512]{1,0:T(8,128)S(1)} %dynamic-slice_bitcast_fusion.2, pred[512,1024]{1,0:T(8,128)(4,1)S(1)} %broadcast_compare_fusion.5, bf16[512,12,64]{0,2,1:T(8,128)(2,1)S(1)} %bitcast.180, ...), kind=kOutput, calls=%fused_computation.18.clone.1 | convolution fusion | flops 836757504 | bytes 53264384 | tf_op jit(solution)/shard_map/while/body/eval_jaxpr/qhd,khd->hqk/dot_general | solution.py:241
  719.0 21.3 %multiply_convert_fusion.6 = bf16[12,512,1024]{2,1,0:T(8,128)(2,1)} fusion(f32[12,512,1024]{2,1,0:T(8,128)} %get-tuple-element.482, f32[12,512,1024]{2,1,0:T(8,128)} %fusion.128, f32[12,512]{1,0:T(8,128)S(1)} %get-tuple-element.483, f32[12,512]{1,0:T(8,128)S(1)} %dynamic-slice_bitcast_fusion.2, pred[512,1024]{1,0:T(8,128)(4,1)S(1)} %broadcast_compare_fusion.5), kind=kLoop, calls=%fused_computation.17.clone.1 | loop fusion | flops 37748736 | bytes 63488000 | tf_op jit(solution)/shard_map/while/body/eval_jaxpr/convert_element_type | solution.py:254
  740.3 9.8 convolution_multiply_fusion.5
  795.2 10.4 fusion.38
  807.6 10.8 fusion.42
  828.5 41.1 %all-reduce.18 = (f32[768]{0:T(1024)S(1)}, f32[768]{0:T(1024)S(1)}, f32[768]{0:T(1024)S(1)}, f32[768]{0:T(1024)S(1)}, f32[768]{0:T(1024)S(1)}, /*index=5*/f32[30...) all-reduce(f32[768]{0:T(1024)S(1)} %convert_reduce_fusion.4, ...), channel_id=7, replica_groups=mesh['dp'=16,'fsdp'=2] {'dp','fsdp'}, use_global_device_ids=true, to_apply=%region_28.29.clone | all-reduce | flops 9216 | bytes 73728
  883.2 97.8 %reduce-scatter.26.cloned.1.call-done = f32[24,768]{1,0:T(8,128)} async-done(((f32[768,768]{1,0:T(8,128)}), f32[24,768]{1,0:T(8,128)}) %reduce-scatter.26.cloned.1.call-update) | async-done | bytes 73744
  981.0 104.5 %reduce-scatter.22.cloned.1.call-done = f32[24,768]{1,0:T(8,128)} async-done(((f32[768,768]{1,0:T(8,128)}), f32[24,768]{1,0:T(8,128)}) %reduce-scatter.22.cloned.1.call-update) | async-done | bytes 73744
  1085.5 141.8 %reduce-scatter.20.cloned.1.call-done = f32[96,768]{1,0:T(8,128)} async-done(((f32[3072,768]{1,0:T(8,128)}), f32[96,768]{1,0:T(8,128)}) %reduce-scatter.20.cloned.1.call-update) | async-done | bytes 294928 | tf_op jit(solution)/shard_map/reduce_scatter | solution.py:220
  1227.3 141.7 %reduce-scatter.18.cloned.1.call-done = f32[24,3072]{1,0:T(8,128)} async-done(((f32[768,3072]{1,0:T(8,128)}), f32[24,3072]{1,0:T(8,128)}) %reduce-scatter.18.cloned.1.call-update) | async-done | bytes 294928 | tf_op jit(solution)/shard_map/reduce_scatter | solution.py:218
  (324 shorter events, 238.4 us)
Async XLA Ops:
  7.2 70.3 %copy-start.16 = (bf16[1,1024,768]{2,1,0:T(8,128)(2,1)S(1)}, bf16[1,1024,768]{2,1,0:T(8,128)(2,1)}, u32[]{:S(2)}) copy-start(bf16[1,1024,768]{2,1,0:T(8,128)(2,1)} %param.25) | copy-start | bytes 4718596
  7.2 69.7 %copy-start.63 = (s32[256]{0:T(256)S(1)}, s32[256]{0:T(256)}, u32[]{:S(2)}) copy-start(s32[256]{0:T(256)} %param.30) | copy-start | bytes 3076
  7.2 70.3 %all-gather.11.cloned.1.call-start = ((), (), s32[]{:S(2)}) async-start(), calls=%async_computation.9 | async-start | bytes 1216512 | tf_op jit(solution)/shard_map/all_gather | solution.py:105
  8.9 115.8 %all-gather.7.cloned.1.call-start = ((), (), s32[]{:S(2)}) async-start(), calls=%async_computation.7 | async-start | bytes 1216512 | tf_op jit(solution)/shard_map/all_gather | solution.py:103
  10.5 170.5 %all-gather.9.cloned.1.call-start = ((), (), s32[]{:S(2)}) async-start(), calls=%async_computation.8 | async-start | bytes 1216512 | tf_op jit(solution)/shard_map/all_gather | solution.py:104
  12.1 255.4 %all-gather.13.cloned.1.call-start = ((), (), s32[]{:S(2)}) async-start(), calls=%async_computation.10 | async-start | bytes 1216512 | tf_op jit(solution)/shard_map/all_gather | solution.py:106
  13.6 289.4 %all-gather.15.cloned.1.call-start = ((), (), s32[]{:S(2)}) async-start(), calls=%async_computation.11 | async-start | bytes 4866048 | tf_op jit(solution)/shard_map/all_gather | solution.py:166
  15.4 353.0 %all-gather.17.cloned.1.call-start = ((), (), s32[]{:S(2)}) async-start(), calls=%async_computation.12 | async-start | bytes 4866048 | tf_op jit(solution)/shard_map/all_gather | solution.py:167
  17.1 509.2 %reduce-scatter.14.cloned.1.call-start = ((), (), s32[]{:S(2)}) async-start(), calls=%async_computation.13 | async-start | bytes 811008 | tf_op jit(solution)/shard_map/reduce_scatter | solution.py:202
  187.9 79.7 %copy-start.52 = (f32[768]{0:T(1024)S(1)}, f32[768]{0:T(1024)}, u32[]{:S(2)}) copy-start(f32[768]{0:T(1024)} %convert_element_type.202) | copy-start | bytes 9220
  201.7 15.4 %copy-start = (f32[12,512,1024]{2,1,0:T(8,128)S(1)}, f32[12,512,1024]{2,1,0:T(8,128)}, u32[]{:S(2)}) copy-start(f32[12,512,1024]{2,1,0:T(8,128)} %get-tuple-element.468) | copy-start | bytes 75497472 | tf_op jit(solution)/shard_map/while
  241.3 15.6 %copy-start = (f32[12,512,1024]{2,1,0:T(8,128)S(1)}, f32[12,512,1024]{2,1,0:T(8,128)}, u32[]{:S(2)}) copy-start(f32[12,512,1024]{2,1,0:T(8,128)} %get-tuple-element.468) | copy-start | bytes 75497472 | tf_op jit(solution)/shard_map/while
  272.0 31.1 %copy-start.37 = (f32[768]{0:T(1024)S(1)}, f32[768]{0:T(1024)}, u32[]{:S(2)}) copy-start(f32[768]{0:T(1024)} %convert_element_type.204) | copy-start | bytes 9220
  272.0 31.1 %copy-start.46 = (f32[3072]{0:T(1024)S(1)}, f32[3072]{0:T(1024)}, u32[]{:S(2)}) copy-start(f32[3072]{0:T(1024)} %convert_element_type.210) | copy-start | bytes 36868
  272.0 31.1 %copy-start.49 = (f32[768]{0:T(1024)S(1)}, f32[768]{0:T(1024)}, u32[]{:S(2)}) copy-start(f32[768]{0:T(1024)} %convert_element_type.206) | copy-start | bytes 9220
  272.1 96.3 %copy-start.34 = (f32[1024]{0:T(1024)}, f32[1024]{0:T(1024)S(1)}, u32[]{:S(2)}) copy-start(f32[1024]{0:T(1024)S(1)} %broadcast_multiply_fusion.5) | copy-start | bytes 12292
  274.1 94.3 %copy-start.40 = (f32[1024]{0:T(1024)}, f32[1024]{0:T(1024)S(1)}, u32[]{:S(2)}) copy-start(f32[1024]{0:T(1024)S(1)} %add_rsqrt_fusion.1) | copy-start | bytes 12292
  274.1 94.3 %copy-start.51 = (f32[768]{0:T(1024)S(1)}, f32[768]{0:T(1024)}, u32[]{:S(2)}) copy-start(f32[768]{0:T(1024)} %convert_element_type.214) | copy-start | bytes 9220
  377.8 160.1 %copy-start.2 = (f32[1024,768]{0,1:T(8,128)}, f32[1024,768]{0,1:T(8,128)S(1)}, u32[]{:S(2)}) copy-start(f32[1024,768]{0,1:T(8,128)S(1)} %get-tuple-element.338) | copy-start | bytes 9437188
  377.9 160.1 %copy-start.24 = (f32[1024]{0:T(1024)}, f32[1024]{0:T(1024)S(1)}, u32[]{:S(2)}) copy-start(f32[1024]{0:T(1024)S(1)} %broadcast_multiply_fusion.4) | copy-start | bytes 12292
  378.6 159.4 %copy-start.28 = (f32[1024]{0:T(1024)}, f32[1024]{0:T(1024)S(1)}, u32[]{:S(2)}) copy-start(f32[1024]{0:T(1024)S(1)} %add_rsqrt_fusion) | copy-start | bytes 12292
  433.7 449.4 %reduce-scatter.16.cloned.1.call-start = ((), (), s32[]{:S(2)}) async-start(), calls=%async_computation.14 | async-start | bytes 2433024 | tf_op jit(solution)/shard_map/reduce_scatter | solution.py:296
  538.0 15.6 %slice-start = ((s8[4718592]{0:T(1024)(128)(4,1)}), s8[4194304]{0:T(1024)(128)(4,1)S(1)}, s32[]{:S(2)}) async-start(s8[4718592]{0:T(1024)(128)(4,1)} %bitcast.193), calls=%async_computation.20 | async-start | bytes 8388608
  539.7 13.9 %copy-start.38 = (f32[768]{0:T(1024)S(1)}, f32[768]{0:T(1024)}, u32[]{:S(2)}) copy-start(f32[768]{0:T(1024)} %convert_element_type.204) | copy-start | bytes 9220
  539.7 13.9 %copy-start.41 = (f32[1024]{0:T(1024)S(1)}, f32[1024]{0:T(1024)}, u32[]{:S(2)}) copy-start(f32[1024]{0:T(1024)} %copy-done.40) | copy-start | bytes 12292
  564.9 318.3 %reduce-scatter.24.cloned.1.call-start = ((), (), s32[]{:S(2)}) async-start(), calls=%async_computation.18 | async-start | bytes 2433024
  777.5 203.4 %reduce-scatter.26.cloned.1.call-start = ((), (), s32[]{:S(2)}) async-start(), calls=%async_computation.19 | async-start | bytes 2433024
  787.5 298.0 %reduce-scatter.22.cloned.1.call-start = ((), (), s32[]{:S(2)}) async-start(), calls=%async_computation.17 | async-start | bytes 2433024
  795.2 432.1 %reduce-scatter.20.cloned.1.call-start = ((), (), s32[]{:S(2)}) async-start(), calls=%async_computation.16 | async-start | bytes 9732096 | tf_op jit(solution)/shard_map/reduce_scatter | solution.py:220
  805.7 563.3 %reduce-scatter.18.cloned.1.call-start = ((), (), s32[]{:S(2)}) async-start(), calls=%async_computation.15 | async-start | bytes 9732096 | tf_op jit(solution)/shard_map/reduce_scatter | solution.py:218
  824.9 49.4 %copy-start.19 = (bf16[1024,768]{0,1:T(8,128)(2,1)S(1)}, bf16[1024,768]{0,1:T(8,128)(2,1)}, u32[]{:S(2)}) copy-start(bf16[1024,768]{0,1:T(8,128)(2,1)} %reduce_sum.217) | copy-start | bytes 4718596
  824.9 49.4 %copy-start.62 = (bf16[768,768]{1,0:T(8,128)(2,1)S(1)}, bf16[768,768]{1,0:T(8,128)(2,1)}, u32[]{:S(2)}) copy-start(bf16[768,768]{1,0:T(8,128)(2,1)} %all-gather.9.cloned.1.call-done) | copy-start | bytes 3538948
  (50 other events, 187.0 us)
Sparse Core Ops, SparseCore 0:
  11.5 56.8 all-gather.10
  71.8 52.7 all-gather.6
  128.1 52.8 all-gather.8
  184.3 52.7 all-gather.12
  240.5 62.5 all-gather.14
  306.4 61.9 all-gather.16
  433.9 92.3 reduce-scatter.13
  565.0 98.7 reduce-scatter.15
  777.6 98.9 reduce-scatter.23
  882.3 98.5 reduce-scatter.25
  986.8 98.6 reduce-scatter.21
  1091.8 135.4 reduce-scatter.19
  1233.8 135.1 reduce-scatter.17
where the time goes:
time: 1380 us
  waiting for transfers between devices  744 us (54%)
  matrix products  272 us (20%)
  other arithmetic  129 us (9%)
  blocking collectives  124 us (9%)
  local copies, waits for them, and re-layouts  88.1 us (6%)
  between operations  14.9 us (1%)
    unnamed x16, waiting for transfers between devices  203 us
    reduce_scatter x1, waiting for transfers between devices, body(): lax.psum_scatter(outer_grad, ('dp', 'fsdp'), scatter_dimension=0, tiled=T...  142 us
    reduce_scatter x1, waiting for transfers between devices, body(): lax.psum_scatter(inner_grad, ('dp', 'fsdp'), scatter_dimension=0, tiled=T...  142 us
    reduce_scatter x1, waiting for transfers between devices, body(): lax.psum_scatter(contract_rows(score_grad, query_emb), ('dp', 'fsdp'), sc...  84 us
    unnamed x2, blocking collectives  83.7 us
    all_gather x1, waiting for transfers between devices, body(): lax.all_gather(w_outer.astype(jnp.bfloat16), ('dp', 'fsdp'), axis=0, tile...  51.6 us
    all_gather x1, waiting for transfers between devices, body(): lax.all_gather(w_key.astype(jnp.bfloat16), ('dp', 'fsdp'), axis=0, tiled=...  50.8 us
    dot_general x4, matrix products, block_scores(): jnp.einsum('qhd,khd->hqk', heads_view(query_block), heads_view(key_row),...  47.6 us
  transfers between devices with their start and end apart: 13, of which 9 were waited for; matrix products, arithmetic and copies ran while one was open for 30% of the time, Pallas kernels for 0%

commit v1 on v0

v1 whole, which is shorter than its diff:
```python
import math

import jax
import jax.numpy as jnp
from jax import lax
from jax.experimental import pallas as pl
from jax.experimental.pallas import tpu as pltpu
from jax.sharding import PartitionSpec as P

HEADS = 12
HEAD = 64
EPS = 1e-12
NEG = -1e30
QB = 128
WINDOWS = (256, 384, 512)
AXES = ("dp", "fsdp")
F32 = jnp.float32
BF16 = jnp.bfloat16


def _bounds(starts_ref, first, last, length):
    low = jnp.int32(0)
    high = jnp.int32(length)
    for s in range(starts_ref.shape[0]):
        at = starts_ref[s]
        low = jnp.maximum(low, jnp.where(at <= first, at, 0))
        high = jnp.minimum(high, jnp.where(at > last, at, length))
    return low, high

def _row_bounds(starts_ref, pos, length):
    low = jnp.zeros_like(pos)
    high = jnp.full_like(pos, length)
    for s in range(starts_ref.shape[0]):
        at = starts_ref[s]
        low = jnp.maximum(low, jnp.where(pos >= at, at, 0))
        high = jnp.minimum(high, jnp.where(pos < at, at, length))
    return low, high

def _variants(starts_ref, length, body):
    first = pl.program_id(0) * QB
    low, high = _bounds(starts_ref, first, first + QB - 1, length)
    base = (low // 16) * 16
    need = high - base
    done = jnp.bool_(False)
    sizes = [w for w in WINDOWS if w < length] + [length]
    prev = 0
    for w in sizes:
        @pl.when(jnp.logical_and(need > prev, need <= w))
        def _(w=w):
            start = pl.multiple_of(jnp.minimum(base, length - w), 16)
            body(w, start, first)
        prev = w

def _pair(block):
    lane = lax.broadcasted_iota(jnp.int32, block.shape, 1)
    zero = jnp.zeros_like(block)
    return jnp.concatenate([jnp.where(lane < HEAD, block, zero), jnp.where(lane < HEAD, zero, block)], axis=0)

def _pick(both):
    half = both.shape[0] // 2
    lane = lax.broadcasted_iota(jnp.int32, (half, both.shape[1]), 1)
    return jnp.where(lane < HEAD, both[:half], both[half:])

def fwd_kernel(starts_ref, q_ref, k_ref, v_ref, c_ref, lse_ref):
    length = k_ref.shape[0]
    def body(w, start, first):
        pos = first + lax.broadcasted_iota(jnp.int32, (QB, 1), 0)
        low, high = _row_bounds(starts_ref, pos, length)
        key = start + lax.broadcasted_iota(jnp.int32, (QB, w), 1)
        bias = jnp.where(jnp.logical_and(key >= low, key < high), 0.0, NEG)
        lane = lax.broadcasted_iota(jnp.int32, (QB, 128), 1)
        lse = jnp.zeros((QB, 128), jnp.float32)
        for h in range(HEADS // 2):
            cols = slice(h * 128, h * 128 + 128)
            q2 = _pair(q_ref[:, cols] * jnp.bfloat16(HEAD ** -0.5))
            kw = k_ref[pl.ds(start, w), cols]
            s = lax.dot_general(q2, kw, (((1,), (1,)), ((), ())), preferred_element_type=jnp.float32)
            s = s + jnp.concatenate([bias, bias], axis=0)
            m = jnp.max(s, axis=-1, keepdims=True)
            e = jnp.exp(s - m)
            l = jnp.sum(e, axis=-1, keepdims=True)
            p = (e * (1.0 / l)).astype(jnp.bfloat16)
            o = jnp.dot(p, v_ref[pl.ds(start, w), cols], preferred_element_type=jnp.float32)
            c_ref[:, cols] = _pick(o).astype(jnp.bfloat16)
            t = m + jnp.log(l)
            lse = jnp.where(lane == 2 * h, t[:QB], lse)
            lse = jnp.where(lane == 2 * h + 1, t[QB:], lse)
        lse_ref[...] = jnp.transpose(lse)[:16]
    _variants(starts_ref, length, body)

def attn_fwd(starts, qkv):
    length = qkv.shape[0]; width = HEADS * HEAD
    return pl.pallas_call(
        fwd_kernel,
        out_shape=(jax.ShapeDtypeStruct((length, width), jnp.bfloat16), jax.ShapeDtypeStruct((16, length), jnp.float32)),
        grid_spec=pltpu.PrefetchScalarGridSpec(
            num_scalar_prefetch=1, grid=(length // QB,),
            in_specs=[pl.BlockSpec((QB, width), lambda i, s: (i, 0)),
                      pl.BlockSpec((length, width), lambda i, s: (0, 1)),
                      pl.BlockSpec((length, width), lambda i, s: (0, 2))],
            out_specs=[pl.BlockSpec((QB, width), lambda i, s: (i, 0)), pl.BlockSpec((16, QB), lambda i, s: (0, i))]),
        compiler_params=pltpu.CompilerParams(dimension_semantics=("arbitrary",), vmem_limit_bytes=48 << 20),
        name="attend",
    )(starts, qkv, qkv, qkv)

def bwd_kernel(starts_ref, q_ref, k_ref, v_ref, dc_ref, lse_ref, out_ref, dk_ref, dv_ref):
    length = k_ref.shape[0]; width = HEADS * HEAD
    step = pl.program_id(0)
    @pl.when(step == 0)
    def _():
        dk_ref[...] = jnp.zeros_like(dk_ref)
        dv_ref[...] = jnp.zeros_like(dv_ref)
    def body(w, start, first):
        pos = first + lax.broadcasted_iota(jnp.int32, (1, QB), 1)
        low, high = _row_bounds(starts_ref, pos, length)
        key = start + lax.broadcasted_iota(jnp.int32, (w, QB), 0)
        bias = jnp.where(jnp.logical_and(key >= low, key < high), 0.0, NEG)
        row = lax.broadcasted_iota(jnp.int32, (128, QB), 0)
        for h in range(HEADS // 2):
            cols = slice(h * 128, h * 128 + 128)
            q2 = _pair(q_ref[:, cols] * jnp.bfloat16(HEAD ** -0.5))
            d2 = _pair(dc_ref[:, cols])
            kw = k_ref[pl.ds(start, w), cols]
            vw = v_ref[pl.ds(start, w), cols]
            s = lax.dot_general(kw, q2, (((1,), (1,)), ((), ())), preferred_element_type=jnp.float32)
            lse = jnp.concatenate([lse_ref[2 * h:2 * h + 1, :], lse_ref[2 * h + 1:2 * h + 2, :]], axis=1)
            p = jnp.exp(s + jnp.concatenate([bias, bias], axis=1) - lse)
            dp = lax.dot_general(vw, d2, (((1,), (1,)), ((), ())), preferred_element_type=jnp.float32)
            delta = jnp.sum(p * dp, axis=0, keepdims=True)
            ds = (p * (dp - delta)).astype(jnp.bfloat16)
            dv_ref[pl.ds(start, w), cols] += jnp.dot(p.astype(jnp.bfloat16), d2, preferred_element_type=jnp.float32)
            dk_ref[pl.ds(start, w), cols] += jnp.dot(ds, q2, preferred_element_type=jnp.float32)
            dqt = lax.dot_general(kw, ds, (((0,), (0,)), ((), ())), preferred_element_type=jnp.float32)
            dqt = jnp.where(row < HEAD, dqt[:, :QB], dqt[:, QB:]) * HEAD ** -0.5
            out_ref[pl.ds(pl.multiple_of(first, QB), QB), cols] = jnp.transpose(dqt).astype(jnp.bfloat16)
    _variants(starts_ref, length, body)
    @pl.when(step == pl.num_programs(0) - 1)
    def _():
        out_ref[:, width:2 * width] = dk_ref[...].astype(jnp.bfloat16)
        out_ref[:, 2 * width:] = dv_ref[...].astype(jnp.bfloat16)

def attn_bwd(starts, qkv, dc, lse):
    length = qkv.shape[0]; width = HEADS * HEAD
    return pl.pallas_call(
        bwd_kernel,
        out_shape=jax.ShapeDtypeStruct((length, 3 * width), jnp.bfloat16),
        grid_spec=pltpu.PrefetchScalarGridSpec(
            num_scalar_prefetch=1, grid=(length // QB,),
            in_specs=[pl.BlockSpec((QB, width), lambda i, s: (i, 0)),
                      pl.BlockSpec((length, width), lambda i, s: (0, 1)),
                      pl.BlockSpec((length, width), lambda i, s: (0, 2)),
                      pl.BlockSpec((QB, width), lambda i, s: (i, 0)),
                      pl.BlockSpec((16, QB), lambda i, s: (0, i))],
            out_specs=pl.BlockSpec((length, 3 * width), lambda i, s: (0, 0)),
            scratch_shapes=[pltpu.VMEM((length, width), jnp.float32), pltpu.VMEM((length, width), jnp.float32)]),
        compiler_params=pltpu.CompilerParams(dimension_semantics=("arbitrary",), vmem_limit_bytes=56 << 20),
        name="attend_back",
    )(starts, qkv, qkv, qkv, dc, lse)


def matmul(left, right):
    return jnp.dot(left, right, preferred_element_type=F32)


def contract_rows(left, right):
    return lax.dot_general(left, right, (((0,), (0,)), ((), ())), preferred_element_type=F32)


def contract_cols(left, right):
    return lax.dot_general(left, right, (((1,), (1,)), ((), ())), preferred_element_type=F32)


def norm_forward(value, gain, shift):
    mean = jnp.mean(value, axis=-1, keepdims=True)
    centred = value - mean
    spread = jnp.mean(centred * centred, axis=-1, keepdims=True)
    scaling = lax.rsqrt(spread + EPS)
    normed = centred * scaling
    return (normed * gain + shift, normed, scaling)


def norm_backward(grad, normed, scaling, gain):
    scaled = grad * gain
    first_mean = jnp.mean(scaled, axis=-1, keepdims=True)
    second_mean = jnp.mean(scaled * normed, axis=-1, keepdims=True)
    result = scaling * (scaled - first_mean - normed * second_mean)
    return (result, jnp.sum(grad * normed, axis=0), jnp.sum(grad, axis=0))


def gelu_parts(pre_act):
    cdf_part = 0.5 * (1.0 + lax.erf(pre_act * (1.0 / math.sqrt(2.0))))
    slope = cdf_part + pre_act * jnp.exp(-0.5 * pre_act * pre_act) * (1.0 / math.sqrt(2.0 * math.pi))
    return (pre_act * cdf_part, slope)


class Cube:
    def __init__(self, chips):
        bits = chips.bit_length() - 1
        side = bits // 3
        self.n = 2 * chips
        self.total = bits + 1
        x_bits = list(range(1, 1 + side))
        y_bits = list(range(1 + side, 1 + 2 * side))
        z_bits = list(range(1 + 2 * side, 1 + bits))
        far = list(reversed(z_bits))
        self.order = [(b, b) for b in far]
        self.order += list(zip(x_bits, y_bits)) + list(zip(y_bits, x_bits))
        self.me = lax.axis_index(AXES)
        self.core = self.me & 1

    def bit(self, pair):
        return (self.me >> jnp.where(self.core == 0, pair[0], pair[1])) & 1

    def swap(self, value, pair):
        perm = [(i, i ^ (1 << pair[i & 1])) for i in range(self.n)]
        return lax.ppermute(value, AXES, perm)

    def gather(self, shard):
        have = shard
        for pair in self.order:
            other = self.swap(have, pair)
            mine_low = self.bit(pair) == 0
            have = jnp.stack([jnp.where(mine_low, have, other), jnp.where(mine_low, other, have)])
        other = self.swap(have, (0, 0))
        mine_low = self.core == 0
        count = len(self.order)
        sides = []
        for side, whole in enumerate((jnp.where(mine_low, have, other), jnp.where(mine_low, other, have))):
            place = {pair[side]: count - 1 - at for at, pair in enumerate(self.order)}
            axes = [place[b] for b in range(self.total - 1, 0, -1)]
            sides.append(jnp.transpose(whole, axes + list(range(count, whole.ndim))))
        whole = jnp.stack(sides, axis=count)
        return whole.reshape((self.n * shard.shape[0],) + shard.shape[1:])

    def scatter(self, grad):
        rows = grad.shape[0] // self.n
        have = grad.reshape((2,) * self.total + (rows,) + grad.shape[1:])
        names = [list(range(self.total - 1, -1, -1))] * 2
        for pair in [(0, 0)] + self.order[::-1]:
            bit = self.bit(pair)
            kept, sent, left = [], [], []
            for side in range(2):
                axis = names[side].index(pair[side])
                kept.append(lax.dynamic_index_in_dim(have, bit, axis, keepdims=False))
                sent.append(lax.dynamic_index_in_dim(have, 1 - bit, axis, keepdims=False))
                left.append(names[side][:axis] + names[side][axis + 1:])
            names = left
            if pair[0] == pair[1] and names[0] == names[1]:
                keep, send = kept[0], sent[0]
            else:
                keep = jnp.where(self.core == 0, kept[0], kept[1])
                send = jnp.where(self.core == 0, sent[0], sent[1])
            have = keep.astype(F32) + self.swap(send.astype(BF16), pair).astype(F32)
        return have


def as_columns(vectors, rows):
    cols = [v.reshape(rows, -1) for v in vectors]
    wide = jnp.concatenate(cols, axis=1)
    return jnp.pad(wide, ((0, 0), (0, 128 - wide.shape[1])))


def body(
    hidden_in,
    row_grad,
    segment_ids,
    query_cls,
    passage_cls,
    positives,
    w_query,
    w_key,
    w_value,
    w_output,
    b_query,
    b_value,
    b_output,
    attn_gain,
    attn_shift,
    w_inner,
    b_inner,
    w_outer,
    b_outer,
    ffn_gain,
    ffn_shift,
    chips,
):
    rows, length, width = hidden_in.shape
    shard = w_query.shape[0]
    cube = Cube(chips)
    inputs = hidden_in.reshape(length, width)
    starts = jnp.stack([query_cls[0], passage_cls[0]], axis=1).reshape(-1)

    vectors = as_columns(
        [b_query, b_value, b_output, attn_gain, attn_shift, b_outer, ffn_gain, ffn_shift, b_inner], shard
    )
    first_shard = jnp.concatenate([w_query, w_key, w_value, vectors], axis=1).astype(BF16)
    hidden = w_inner.shape[1]
    rest_shard = jnp.concatenate([w_output, w_inner, w_outer.reshape(shard, -1)], axis=1).astype(BF16)
    first = cube.gather(first_shard)
    rest = lax.all_gather(rest_shard, AXES, axis=0, tiled=True)
    qkv_mat = first[:, : 3 * width]
    small = first[:, 3 * width :].astype(F32).T
    query_bias, value_bias, output_bias, gain_one, shift_one, outer_bias, gain_two, shift_two = small[:8]
    inner_bias = small[8 : 8 + hidden // width].T.reshape(-1)
    qkv_bias = jnp.concatenate([query_bias, jnp.zeros_like(query_bias), value_bias])
    qkv = (matmul(inputs, qkv_mat) + qkv_bias).astype(BF16)
    context, lse = attn_fwd(starts, qkv)

    output_mat = rest[:, :width]
    inner_mat = rest[:, width : width + hidden]
    outer_mat = rest[:, width + hidden :].reshape(hidden, width)
    branch = matmul(context, output_mat) + output_bias
    middle, normed_one, scaling_one = norm_forward(inputs.astype(F32) + branch, gain_one, shift_one)
    middle_low = middle.astype(BF16)
    pre_act = matmul(middle_low, inner_mat) + inner_bias
    activated, slope = gelu_parts(pre_act)
    act_low = activated.astype(BF16)
    update = matmul(act_low, outer_mat) + outer_bias
    output, normed_two, scaling_two = norm_forward(middle + update, gain_two, shift_two)
    output_low = output.astype(BF16)

    pairs = query_cls.shape[1]
    cls = jnp.concatenate([query_cls[0], passage_cls[0]])
    pick = cls[:, None] == jnp.arange(length, dtype=jnp.int32)[None, :]
    own = matmul(pick.astype(BF16), output_low).astype(BF16)
    everyone = cube.gather(own[None])
    count = everyone.shape[0] * pairs
    all_queries = everyone[:, :pairs].reshape(count, width)
    all_passages = everyone[:, pairs:].reshape(count, width)
    score_scale = 4.0 / math.sqrt(width)
    scores = contract_cols(all_queries, all_passages) * score_scale
    hit = (jnp.arange(count, dtype=jnp.int32)[None, :] == positives[:, None]).astype(F32)
    highest = jnp.max(scores, axis=-1, keepdims=True)
    log_total = highest + jnp.log(jnp.sum(jnp.exp(scores - highest), axis=-1, keepdims=True))
    losses = log_total[:, 0] - jnp.sum(hit * scores, axis=-1)
    score_grad = ((jnp.exp(scores - log_total) - hit) * score_scale).astype(BF16)
    begin = cube.me * pairs
    query_loss = lax.dynamic_slice_in_dim(losses, begin, pairs, 0)
    own_rows = lax.dynamic_slice_in_dim(score_grad, begin, pairs, 0)
    own_cols = lax.dynamic_slice_in_dim(score_grad, begin, pairs, 1)
    cls_grad = jnp.concatenate([matmul(own_rows, all_passages), contract_rows(own_cols, all_queries)])
    added = jnp.einsum("nt,nd->td", pick.astype(F32), cls_grad, precision=lax.Precision.HIGHEST)
    out_grad = row_grad.reshape(length, width).astype(F32) + added

    sum_grad, gain_two_grad, shift_two_grad = norm_backward(out_grad, normed_two, scaling_two, gain_two)
    update_grad = sum_grad.astype(BF16)
    outer_grad = contract_rows(act_low, update_grad).astype(BF16)
    outer_bias_grad = jnp.sum(update_grad.astype(F32), axis=0)
    w_outer_grad = cube.scatter(outer_grad)
    pre_grad = (contract_cols(update_grad, outer_mat) * slope).astype(BF16)
    inner_grad = contract_rows(middle_low, pre_grad).astype(BF16)
    inner_bias_grad = jnp.sum(pre_grad.astype(F32), axis=0)
    w_inner_grad = cube.scatter(inner_grad)
    middle_grad = sum_grad + contract_cols(pre_grad, inner_mat)
    first_grad, gain_one_grad, shift_one_grad = norm_backward(middle_grad, normed_one, scaling_one, gain_one)
    branch_grad = first_grad.astype(BF16)
    output_bias_grad = jnp.sum(branch_grad.astype(F32), axis=0)
    output_w_grad = contract_rows(context, branch_grad).astype(BF16)
    context_grad = contract_cols(branch_grad, output_mat).astype(BF16)

    qkv_grad = attn_bwd(starts, qkv, context_grad, lse)
    qkv_w_grad = contract_rows(inputs, qkv_grad).astype(BF16)
    qkv_bias_grad = jnp.sum(qkv_grad.astype(F32), axis=0)
    hidden_grad = first_grad + contract_cols(qkv_grad, qkv_mat)
    vector_grads = as_columns(
        [
            qkv_bias_grad[:width],
            qkv_bias_grad[2 * width :],
            output_bias_grad,
            gain_one_grad,
            shift_one_grad,
            outer_bias_grad,
            gain_two_grad,
            shift_two_grad,
            inner_bias_grad,
        ],
        width,
    )
    last = cube.scatter(jnp.concatenate([qkv_w_grad, output_w_grad, vector_grads.astype(BF16)], axis=1))
    tail = last[:, 4 * width :]
    vec = [tail[:, j] for j in range(8)]
    return (
        query_loss,
        output_low[None],
        hidden_grad[None],
        last[:, :width],
        last[:, width : 2 * width],
        last[:, 2 * width : 3 * width],
        last[:, 3 * width : 4 * width],
        vec[0],
        vec[1],
        vec[2],
        vec[3],
        vec[4],
        w_inner_grad,
        tail[:, 8 : 8 + hidden // width].reshape(-1),
        w_outer_grad,
        vec[5],
        vec[6],
        vec[7],
    )


def solution(mesh):
    rows3 = P(AXES, None, None)
    rows2 = P(AXES, None)
    rows1 = P(AXES)
    chips = mesh.shape["dp"]

    def run(*args):
        return body(*args, chips=chips)

    return jax.shard_map(
        run,
        mesh=mesh,
        in_specs=(rows3, rows3, rows2, rows2, rows2, P())
        + (rows2,) * 4
        + (rows1,) * 5
        + (rows2, rows1, rows2)
        + (rows1,) * 3,
        out_specs=(rows1, rows3, rows3)
        + (rows2,) * 4
        + (rows1,) * 5
        + (rows2, rows1, rows2)
        + (rows1,) * 3,
        check_vma=False,
    )
```

time: 1380 us -> 437 us (0.32)
  waiting for transfers between devices: 744 us -> 130 us
  matrix products: 272 us -> 94 us
  blocking collectives: 124 us -> 0 us
  other arithmetic: 129 us -> 51.3 us
  Pallas kernels: 0 us -> 38.9 us
  starting transfers between devices: 0.54 us -> 37.1 us
  local copies, waits for them, and re-layouts: 88.1 us -> 62.3 us
    reduce_scatter x4 -> x0, waiting for transfers between devices: 367 us -> none  [the longest x1 142 us: body(): lax.psum_scatter(outer_grad, ('dp', 'fsdp'), scatter_dimension=0, tiled=T...]
    unnamed x16 -> x1, waiting for transfers between devices: 203 us -> 0.02 us
    all_gather x6 -> x1, waiting for transfers between devices: 174 us -> 0.01 us  [body(): rest = lax.all_gather(rest_shard, AXES, axis=0, tiled=True)]
    dot_general x21 -> x7, matrix products: 206 us -> 33.4 us  [the longest x6 30 us: matmul(): return jnp.dot(left, right, preferred_element_type=F32)]
    ppermute x0 -> x25, waiting for transfers between devices: none -> 130 us  [swap(): return lax.ppermute(value, AXES, perm)]
    unnamed x2 -> x0, blocking collectives: 83.7 us -> none
    convert_element_type x28 -> x4, other arithmetic: 67.7 us -> 0.99 us  [the longest x3 0.91 us: scatter(): have = keep.astype(F32) + self.swap(send.astype(BF16), pair).astype(F32)]
    all_gather x1 -> x0, blocking collectives: 40.1 us -> none  [body(): lax.all_gather(passage_emb, ('dp', 'fsdp'), axis=0, tiled=True)]
  transfers between devices with their start and end apart: 13 -> 26, of which waited for: 9 -> 17; matrix products, arithmetic and copies ran while one was open for 30% -> 20% of each run, Pallas kernels for 0% -> 4%
where the time goes in v1:
time: 437 us; the launch traced here: 429 us
  waiting for transfers between devices  130 us (30%)
  matrix products  94 us (22%)
  local copies, waits for them, and re-layouts  62.3 us (14%)
  other arithmetic  51.3 us (12%)
  Pallas kernels  38.9 us (9%)
  starting transfers between devices  37.1 us (8%)
  between operations  15.2 us (3%)
    ppermute x25, waiting for transfers between devices, swap(): return lax.ppermute(value, AXES, perm)  130 us
    ppermute x25, starting transfers between devices, swap(): return lax.ppermute(value, AXES, perm)  37.1 us
    dot_general x5, matrix products, contract_cols(): lax.dot_general(left, right, (((1,), (1,)), ((), ())), preferred_element_...  34.5 us
    dot_general x6, matrix products, matmul(): return jnp.dot(left, right, preferred_element_type=F32)  30 us
    dot_general x5, matrix products, contract_rows(): lax.dot_general(left, right, (((0,), (0,)), ((), ())), preferred_element_...  26.1 us
    pallas_call x1, Pallas kernels, attn_bwd(): pl.pallas_call(bwd_kernel, out_shape=jax.ShapeDtypeStruct((length, 3 * wi...  23.5 us
    pallas_call x1, Pallas kernels, attn_fwd(): pl.pallas_call(fwd_kernel, out_shape=(jax.ShapeDtypeStruct((length, width...  15.4 us
    unnamed x104, local copies, waits for them, and re-layouts  15.2 us
  transfers between devices with their start and end apart: 26, of which 17 were waited for; matrix products, arithmetic and copies ran while one was open for 20% of the time, Pallas kernels for 4%

profile of v1, /device:TPU:0, one launch (start us, length us, event | category | flops | bytes accessed | tf_op | source)
XLA Modules:
  0.0 429.0 jit_solution(9566470983032786333)
XLA Ops:
  20.6 4.1 collective-permute-start
  24.8 11.0 %collective-permute-done = bf16[24,2432]{1,0:T(8,128)(2,1)S(1)} collective-permute-done((bf16[24,2432]{1,0:T(8,128)(2,1)S(1)}, bf16[24,2432]{1,0:T(8,128)(2,1)S(1)}, u32[]{:S(2)}, u32[]{:S(2)}) %collective-permute-start) | collective-permute-done | bytes 116768 | tf_op jit(solution)/shard_map/ppermute | solution.py:216
  35.9 6.6 %collective-permute-done.1 = bf16[2,24,2432]{2,1,0:T(8,128)(2,1)S(1)} collective-permute-done((bf16[2,24,2432]{2,1,0:T(8,128)(2,1)S(1)}, bf16[2,24,2432]{2,1,0:T(8,128)(2,1)S(1)}, u32[]{:S(2)}, u32[]{:S(2)}) %collective-permute-start.1) | collective-permute-done | bytes 233504 | tf_op jit(solution)/shard_map/ppermute | solution.py:216
  44.2 17.5 %collective-permute-done.2 = bf16[2,2,24,2432]{3,2,0,1:T(8,128)(2,1)S(1)} collective-permute-done((bf16[2,2,24,2432]{3,2,0,1:T(8,128)(2,1)S(1)}, bf16[2,2,24,2432]{3,2,0,1:T(8,128)(2,1)S(1)}, u32[]{:S(2)}, u32[]{:S(2)}) %collective-permute-start.2) | collective-permute-done | bytes 466976 | tf_op jit(solution)/shard_map/ppermute | solution.py:216
  63.0 12.7 %collective-permute-done.3 = bf16[2,2,2,24,2432]{4,3,0,1,2:T(8,128)(2,1)} collective-permute-done((bf16[2,2,2,24,2432]{4,3,0,1,2:T(8,128)(2,1)S(1)}, bf16[2,2,2,24,2432]{4,3,0,1,2:T(8,128)(2,1)}, u32[]{:S(2)}, u32[]{:S(2)}) %collective-permute-start.3) | collective-permute-done | bytes 933920 | tf_op jit(solution)/shard_map/ppermute | solution.py:216
  89.1 7.5 %fusion.8.q_ref.k_ref.v_ref = bf16[1024,2304]{1,0:T(8,128)(2,1)} fusion(f32[2304]{0:T(1024)S(1)} %pad_maximum_fusion.11, bf16[768,2432]{1,0:T(8,128)(2,1)} %bitcast.260, bf16[1,1024,768]{2,1,0:T(8,128)(2,1)S(1)} %copy-done.13), kind=kOutput, calls=%fused_computation.17 | convolution fusion | flops 3628597248 | bytes 9839616 | tf_op jit(solution)/shard_map/dot_general | solution.py:162
  96.6 15.4 %attend.1 = (bf16[1024,768]{1,0:T(8,128)(2,1)S(1)}, f32[16,1024]{1,0:T(8,128)S(1)}) custom-call(s32[16]{0:T(128)S(1)} %reshape.217.starts_ref, bf16[1024,2304]{1,0:T(8,128)(2,1)} %fusion.8.q_ref.k_ref.v_ref, bf16[1024,2304]{1,0:T(8,128)(2,1)} %fusion.8.q_ref.k_ref.v_ref, bf16[1024,2304]{1,0:T(8,128)(2,1)} %fusion.8.q_ref.k_ref.v_ref), custom_call_target="tpu_custom_call" | custom-call | tf_op jit(solution)/shard_map/attend/pallas_call | solution.py:93
  117.7 4.9 %slice.118 = bf16[768,3072]{1,0:T(8,128)(2,1)} slice(bf16[768,6912]{1,0:T(8,128)(2,1)} %all-gather.2.cloned.1.call-done), slice={[0:768], [3840:6912]} | slice | bytes 9437184 | tf_op jit(solution)/shard_map/slice | solution.py:311
  122.6 8.9 %reshape.229 = bf16[3072,768]{1,0:T(8,128)(2,1)} reshape(bf16[768,3072]{1,0:T(8,128)(2,1)} %slice.118) | data formatting | bytes 9437184 | tf_op jit(solution)/shard_map/reshape | solution.py:311
  131.4 12.7 %multiply_convert_fusion = (bf16[1024,3072]{1,0:T(8,128)(2,1)S(1)}, f32[1024,3072]{1,0:T(8,128)}) fusion(f32[3072]{0:T(1024)S(1)} %add.261, bf16[768,6912]{1,0:T(8,128)(2,1)} %all-gather.2.cloned.1.call-done, f32[1024,768]{0,1:T(8,128)} %copy-done.4, f32[768]{0:T(1024)S(1)} %get-tuple-element.87, f32[768]{0:T(1024)S(1)} %get-tuple-element.88, ...), kind=kOutput, calls=%fused_computation.7 | convolution fusion | flops 4854644736 | bytes 26765312 | tf_op jit(solution)/shard_map/dot_general | solution.py:162
  144.2 5.8 %fusion.72 = (f32[1024]{0:T(1024)S(1)}, f32[1024,768]{0,1:T(8,128)S(1)}) fusion(f32[768]{0:T(1024)S(1)} %get-tuple-element.86, bf16[1024,3072]{1,0:T(8,128)(2,1)S(1)} %get-tuple-element.128, bf16[3072,768]{1,0:T(8,128)(2,1)S(1)} %copy-done.7, f32[768]{0:T(1024)S(1)} %get-tuple-element.87, f32[768]{0:T(1024)S(1)} %get-tuple-element.88, ...), kind=kOutput, calls=%fused_computation.214 | convolution fusion | flops 4837342208 | bytes 17323008 | tf_op jit(solution)/shard_map/dot_general | solution.py:162
  156.6 5.1 %collective-permute-start.6 = (bf16[2,1,16,768]{3,2,0,1:T(8,128)(2,1)S(1)}, bf16[2,1,16,768]{3,2,0,1:T(8,128)(2,1)S(1)}, u32[]{:S(2)}, u32[]{:S(2)}) collective-permute-start(bf16[2,1,16,768]{3,2,0,1:T(8,128)(2,1)S(1)} %fusion.59), channel_id=1, source_target_pairs={{0,8},{1,9},{2,10},{3,11},{4,12},{5,13},{6,14},{7,15},{8,0},{9,1},... | collective-permute-start | bytes 147464 | tf_op jit(solution)/shard_map/ppermute | solution.py:216
  164.5 4.1 collective-permute-done.7
  171.8 3.6 collective-permute-done.8
  185.7 3.4 multiply_reduce_fusion
  190.9 7.0 %convolution_convert_fusion = bf16[3072,768]{1,0:T(8,128)(2,1)} fusion(bf16[1024,3072]{1,0:T(8,128)(2,1)S(1)} %bitcast.272, f32[1024,768]{0,1:T(8,128)S(1)} %get-tuple-element.103), kind=kOutput, calls=%fused_computation.12 | convolution fusion | flops 4834983936 | bytes 14155776 | tf_op jit(solution)/shard_map/dot_general | solution.py:166
  198.0 14.9 %fusion.74 = (bf16[3072]{0:T(1024)(128)(2,1)}, bf16[1024,3072]{1,0:T(8,128)(2,1)}) fusion(f32[1024,3072]{1,0:T(8,128)} %get-tuple-element.129, f32[3072]{0:T(1024)S(1)} %copy-done.23, bf16[3072,768]{1,0:T(8,128)(2,1)S(1)} %bitcast.252, f32[1024,768]{0,1:T(8,128)S(1)} %get-tuple-element.103), kind=kOutput, calls=%fused_computation.216 | convolution fusion | flops 4870370304 | bytes 26757120 | tf_op jit(solution)/shard_map/dot_general | solution.py:170
  212.9 9.8 %convolution_convert_fusion.1 = bf16[768,3072]{1,0:T(8,128)(2,1)} fusion(bf16[1024,3072]{1,0:T(8,128)(2,1)} %get-tuple-element.137, f32[1024,768]{0,1:T(8,128)S(1)} %copy-done.6, f32[768]{0:T(1024)S(1)} %copy-done.27, f32[768]{0:T(1024)S(1)} %copy-done.19, f32[1024]{0:T(1024)S(1)} %copy-done.21, f32[1024]{0:T(1024)S(1)} %broadcast_multiply_fusion.5), kind=kOutput, calls=%fused_computation.13 | convolution fusion | flops 4838129664 | bytes 14170112 | tf_op jit(solution)/shard_map/dot_general | solution.py:166
  222.7 8.9 %multiply_reduce_fusion.1 = (bf16[768]{0:T(1024)(128)(2,1)}, f32[1024]{0:T(1024)S(1)}, f32[1024]{0:T(1024)S(1)}, bf16[768]{0:T(1024)(128)(2,1)}, f32[1024,768]{0,1:T(8,128)S(1)}) fusion(f32[1024,768]{0,1:T(8,128)S(1)} %copy-done.6, f32[1024]{0:T(1024)S(1)} %copy-done.21, f32[1024]{0:T(1024)S(1)} %broadcast_multiply_fusion.5, f32[768]{0:T(1024)S(1)} %copy-done.19, ...), kind=kOutput, calls=%fused_computation.28 | convolution fusion | flops 4839698432 | bytes 20470784 | tf_op jit(solution)/shard_map/dot_general | solution.py:170
  238.3 23.5 %attend_back.1 = bf16[1024,2304]{1,0:T(8,128)(2,1)} custom-call(s32[16]{0:T(128)} %copy-done.1, bf16[1024,2304]{1,0:T(8,128)(2,1)} %fusion.8.q_ref.k_ref.v_ref, bf16[1024,2304]{1,0:T(8,128)(2,1)} %fusion.8.q_ref.k_ref.v_ref, bf16[1024,2304]{1,0:T(8,128)(2,1)} %fusion.8.q_ref.k_ref.v_ref, bf16[1024,768]{1,0:T(8,128)(2,1)} %convolution_convert_fusion.3.dc_ref, ...), custom_call_target="tpu_custom_call" | custom-call | tf_op jit(solution)/shard_map/attend_back/pallas_call | solution.py:144
  261.8 6.7 %fusion.9 = bf16[768,2304]{0,1:T(8,128)(2,1)S(1)} fusion(bf16[1024,2304]{1,0:T(8,128)(2,1)} %attend_back.1, bf16[1,1024,768]{2,1,0:T(8,128)(2,1)S(1)} %copy-done.14), kind=kOutput, calls=%fused_computation.20 | convolution fusion | flops 3625648128 | bytes 9830400 | tf_op jit(solution)/shard_map/dot_general | solution.py:166
  289.7 9.5 %fusion.7 = bf16[768,3200]{0,1:T(8,128)(2,1)} fusion(bf16[768,12]{0,1:T(8,128)(2,1)} %concatenate.34, bf16[768,768]{0,1:T(8,128)(2,1)} %convolution_convert_fusion.4, bf16[768,2304]{0,1:T(8,128)(2,1)S(1)} %fusion.9), kind=kLoop, calls=%fused_computation.15 | loop fusion | flops 19660800 | bytes 9652224 | tf_op jit(solution)/shard_map/concatenate | solution.py:379
  299.8 7.6 %copy.175 = bf16[768,3200]{1,0:T(8,128)(2,1)} copy(bf16[768,3200]{0,1:T(8,128)(2,1)} %fusion.7) | data formatting | bytes 9830400 | tf_op jit(solution)/shard_map/concatenate | solution.py:379
  307.4 3.4 dynamic-slice_bitcast_fusion
  311.3 7.8 %add_bitcast_fusion = f32[1,1024,768]{1,2,0:T(8,128)} fusion(f32[1024,768]{0,1:T(8,128)S(1)} %copy-done.11, bf16[1024,2304]{1,0:T(8,128)(2,1)} %attend_back.1, bf16[768,2432]{1,0:T(8,128)(2,1)S(1)} %bitcast.261), kind=kOutput, calls=%fused_computation.29 | convolution fusion | flops 3624665088 | bytes 14548992 | tf_op jit(solution)/shard_map/dot_general | solution.py:170
  319.2 3.8 copy.185
  335.0 7.7 %collective-permute-done.21 = bf16[2,2,2,96,768]{4,3,0,1,2:T(8,128)(2,1)S(1)} collective-permute-done((bf16[2,2,2,96,768]{4,3,0,1,2:T(8,128)(2,1)S(1)}, bf16[2,2,2,96,768]{4,3,0,1,2:T(8,128)(2,1)S(1)}, u32[]{:S(2)}, u32[]{:S(2)}) %collective-permute-start.21) | collective-permute-done | bytes 1179680 | tf_op jit(solution)/shard_map/ppermute | solution.py:216
  344.7 16.9 %collective-permute-done.16 = bf16[2,2,2,24,3072]{4,3,0,1,2:T(8,128)(2,1)S(1)} collective-permute-done((bf16[2,2,2,24,3072]{4,3,0,1,2:T(8,128)(2,1)S(1)}, bf16[2,2,2,24,3072]{4,3,0,1,2:T(8,128)(2,1)S(1)}, u32[]{:S(2)}, u32[]{:S(2)}) %collective-permute-start.16) | collective-permute-done | bytes 1179680 | tf_op jit(solution)/shard_map/ppermute | solution.py:216
  363.9 17.2 %collective-permute-done.11 = bf16[2,2,2,24,3200]{4,3,2,1,0:T(8,128)(2,1)S(1)} collective-permute-done((bf16[2,2,2,24,3200]{4,3,2,1,0:T(8,128)(2,1)S(1)}, bf16[2,2,2,24,3200]{4,3,2,1,0:T(8,128)(2,1)S(1)}, u32[]{:S(2)}, u32[]{:S(2)}) %collective-permute-start.11) | collective-permute-done | bytes 1228832 | tf_op jit(solution)/shard_map/ppermute | solution.py:216
  385.6 6.1 %collective-permute-done.12 = bf16[2,2,24,3200]{3,2,1,0:T(8,128)(2,1)S(1)} collective-permute-done((bf16[2,2,24,3200]{3,2,1,0:T(8,128)(2,1)S(1)}, bf16[2,2,24,3200]{3,2,1,0:T(8,128)(2,1)S(1)}, u32[]{:S(2)}, u32[]{:S(2)}) %collective-permute-start.12) | collective-permute-done | bytes 614432 | tf_op jit(solution)/shard_map/ppermute | solution.py:216
  393.4 6.1 %collective-permute-done.18 = bf16[2,24,3072]{2,1,0:T(8,128)(2,1)S(1)} collective-permute-done((bf16[2,24,3072]{2,1,0:T(8,128)(2,1)S(1)}, bf16[2,24,3072]{2,1,0:T(8,128)(2,1)S(1)}, u32[]{:S(2)}, u32[]{:S(2)}) %collective-permute-start.18) | collective-permute-done | bytes 294944 | tf_op jit(solution)/shard_map/ppermute | solution.py:216
  402.8 9.9 %collective-permute-done.19 = bf16[24,3072]{1,0:T(8,128)(2,1)S(1)} collective-permute-done((bf16[24,3072]{1,0:T(8,128)(2,1)S(1)}, bf16[24,3072]{1,0:T(8,128)(2,1)S(1)}, u32[]{:S(2)}, u32[]{:S(2)}) %collective-permute-start.19) | collective-permute-done | bytes 147488 | tf_op jit(solution)/shard_map/ppermute | solution.py:216
  (280 shorter events, 123.5 us)
Async XLA Ops:
  7.2 105.5 %all-gather.2.cloned.1.call-start = ((), (), s32[]{:S(2)}) async-start(), calls=%async_computation | async-start | bytes 10948608 | tf_op jit(solution)/shard_map/all_gather | solution.py:300
  20.6 15.1 %collective-permute-start = (bf16[24,2432]{1,0:T(8,128)(2,1)S(1)}, bf16[24,2432]{1,0:T(8,128)(2,1)S(1)}, u32[]{:S(2)}, u32[]{:S(2)}) collective-permute-start(bf16[24,2432]{1,0:T(8,128)(2,1)S(1)} %fusion.49), channel_id=1, source_target_pairs={{0,16},{1,17},{2,18},{3,19},{4,20},{5,21},{6,22},{7,23},{8,24},{9,... | collective-permute-start | bytes 350216 | tf_op jit(solution)/shard_map/ppermute | solution.py:216
  35.8 6.7 %collective-permute-start.1 = (bf16[2,24,2432]{2,1,0:T(8,128)(2,1)S(1)}, bf16[2,24,2432]{2,1,0:T(8,128)(2,1)S(1)}, u32[]{:S(2)}, u32[]{:S(2)}) collective-permute-start(bf16[2,24,2432]{2,1,0:T(8,128)(2,1)S(1)} %pad_maximum_fusion.7), channel_id=1, source_target_pairs={{0,8},{1,9},{2,10},{3,11},{4,12},{5,13},{6,14},{7,15},{8,0},{9,1},... | collective-permute-start | bytes 700424 | tf_op jit(solution)/shard_map/ppermute | solution.py:216
  42.7 19.1 %collective-permute-start.2 = (bf16[2,2,24,2432]{3,2,0,1:T(8,128)(2,1)S(1)}, bf16[2,2,24,2432]{3,2,0,1:T(8,128)(2,1)S(1)}, u32[]{:S(2)}, u32[]{:S(2)}) collective-permute-start(bf16[2,2,24,2432]{3,2,0,1:T(8,128)(2,1)S(1)} %pad_maximum_fusion.4), channel_id=1, source_target_pairs={{0,2},{1,5},{2,0},{3,7},{4,6},{5,1},{6,4},{7,3},{8,10},{9,13},{10,... | collective-permute-start | bytes 1400840 | tf_op jit(solution)/shard_map/ppermute | solution.py:216
  62.0 13.7 %collective-permute-start.3 = (bf16[2,2,2,24,2432]{4,3,0,1,2:T(8,128)(2,1)S(1)}, bf16[2,2,2,24,2432]{4,3,0,1,2:T(8,128)(2,1)}, u32[]{:S(2)}, u32[]{:S(2)}) collective-permute-start(bf16[2,2,2,24,2432]{4,3,0,1,2:T(8,128)(2,1)S(1)} %pad_maximum_fusion.2), channel_id=1, source_target_pairs={{0,4},{1,3},{2,6},{3,1},{4,0},{5,7},{6,2},{7,5},{8,12},{9,11},{10,... | collective-permute-start | bytes 2801672 | tf_op jit(solution)/shard_map/ppermute | solution.py:216
  78.5 4.3 %collective-permute-start.4 = (bf16[2,2,2,2,24,2432]{5,4,0,1,2,3:T(8,128)(2,1)}, bf16[2,2,2,2,24,2432]{5,4,0,1,2,3:T(8,128)(2,1)}, u32[]{:S(2)}, u32[]{:S(2)}) collective-permute-start(bf16[2,2,2,2,24,2432]{5,4,0,1,2,3:T(8,128)(2,1)} %pad_maximum_fusion.1), channel_id=1, source_target_pairs={{0,1},{1,0},{2,3},{3,2},{4,5},{5,4},{6,7},{7,6},{8,9},{9,8},{10,11... | collective-permute-start | bytes 5603336 | tf_op jit(solution)/shard_map/ppermute | solution.py:216
  81.4 69.1 %copy-start.36 = (s32[16]{0:T(128)}, s32[16]{0:T(128)S(1)}, u32[]{:S(2)}) copy-start(s32[16]{0:T(128)S(1)} %pad_add_fusion.1) | copy-start | bytes 196
  87.4 44.0 %copy-start.22 = (f32[3072]{0:T(1024)}, f32[3072]{0:T(1024)S(1)}, u32[]{:S(2)}) copy-start(f32[3072]{0:T(1024)S(1)} %add.261) | copy-start | bytes 36868
  89.0 55.1 %copy-start.18 = (f32[768]{0:T(1024)}, f32[768]{0:T(1024)S(1)}, u32[]{:S(2)}) copy-start(f32[768]{0:T(1024)S(1)} %get-tuple-element.88) | copy-start | bytes 9220
  89.1 55.1 %copy-start.26 = (f32[768]{0:T(1024)}, f32[768]{0:T(1024)S(1)}, u32[]{:S(2)}) copy-start(f32[768]{0:T(1024)S(1)} %get-tuple-element.87) | copy-start | bytes 9220
  89.1 61.4 %copy-start.17 = (f32[768]{0:T(1024)}, f32[768]{0:T(1024)S(1)}, u32[]{:S(2)}) copy-start(f32[768]{0:T(1024)S(1)} %get-tuple-element.85) | copy-start | bytes 9220
  151.7 4.9 %collective-permute-start.5 = (bf16[1,16,768]{2,1,0:T(8,128)(2,1)S(1)}, bf16[1,16,768]{2,1,0:T(8,128)(2,1)S(1)}, u32[]{:S(2)}, u32[]{:S(2)}) collective-permute-start(bf16[1,16,768]{2,1,0:T(8,128)(2,1)S(1)} %fusion.31), channel_id=1, source_target_pairs={{0,16},{1,17},{2,18},{3,19},{4,20},{5,21},{6,22},{7,23},{8,24},{9,... | collective-permute-start | bytes 73736 | tf_op jit(solution)/shard_map/ppermute | solution.py:216
  156.6 7.2 %collective-permute-start.6 = (bf16[2,1,16,768]{3,2,0,1:T(8,128)(2,1)S(1)}, bf16[2,1,16,768]{3,2,0,1:T(8,128)(2,1)S(1)}, u32[]{:S(2)}, u32[]{:S(2)}) collective-permute-start(bf16[2,1,16,768]{3,2,0,1:T(8,128)(2,1)S(1)} %fusion.59), channel_id=1, source_target_pairs={{0,8},{1,9},{2,10},{3,11},{4,12},{5,13},{6,14},{7,15},{8,0},{9,1},... | collective-permute-start | bytes 147464 | tf_op jit(solution)/shard_map/ppermute | solution.py:216
  163.9 4.8 %collective-permute-start.7 = (bf16[2,2,1,16,768]{4,3,1,0,2:T(8,128)(2,1)S(1)}, bf16[2,2,1,16,768]{4,3,1,0,2:T(8,128)(2,1)S(1)}, u32[]{:S(2)}, u32[]{:S(2)}) collective-permute-start(bf16[2,2,1,16,768]{4,3,1,0,2:T(8,128)(2,1)S(1)} %fusion.52), channel_id=1, source_target_pairs={{0,2},{1,5},{2,0},{3,7},{4,6},{5,1},{6,4},{7,3},{8,10},{9,13},{10,... | collective-permute-start | bytes 294920 | tf_op jit(solution)/shard_map/ppermute | solution.py:216
  168.8 6.7 %collective-permute-start.8 = (bf16[2,2,2,1,16,768]{5,4,2,1,0,3:T(8,128)(2,1)S(1)}, bf16[2,2,2,1,16,768]{5,4,2,1,0,3:T(8,128)(2,1)S(1)}, u32[]{:S(2)}, u32[]{:S(2)}) collective-permute-start(bf16[2,2,2,1,16,768]{5,4,2,1,0,3:T(8,128)(2,1)S(1)} %fusion.48), channel_id=1, source_target_pairs={{0,4},{1,3},{2,6},{3,1},{4,0},{5,7},{6,2},{7,5},{8,12},{9,11},{10,... | collective-permute-start | bytes 589832 | tf_op jit(solution)/shard_map/ppermute | solution.py:216
  176.4 5.8 %collective-permute-start.9 = (bf16[2,2,2,2,1,16,768]{6,5,3,2,0,1,4:T(8,128)(2,1)}, bf16[2,2,2,2,1,16,768]{6,5,3,2,0,1,4:T(8,128)(2,1)}, u32[]{:S(2)}, u32[]{:S(2)}) collective-permute-start(bf16[2,2,2,2,1,16,768]{6,5,3,2,0,1,4:T(8,128)(2,1)} %copy.166), channel_id=1, source_target_pairs={{0,1},{1,0},{2,3},{3,2},{4,5},{5,4},{6,7},{7,6},{8,9},{9,8},{10,11... | collective-permute-start | bytes 1179656 | tf_op jit(solution)/shard_map/ppermute | solution.py:216
  190.9 31.8 %slice-start.6 = ((s8[10616832]{0:T(1024)(128)(4,1)}), s8[4194304]{0:T(1024)(128)(4,1)S(1)}, s32[]{:S(2)}) async-start(s8[10616832]{0:T(1024)(128)(4,1)} %bitcast.265), calls=%async_computation.7 | async-start | bytes 8388608
  278.2 44.8 %collective-permute-start.20 = (bf16[2,2,2,2,96,768]{5,4,3,2,1,0:T(8,128)(2,1)}, bf16[2,2,2,2,96,768]{5,4,3,2,1,0:T(8,128)(2,1)}, u32[]{:S(2)}, u32[]{:S(2)}) collective-permute-start(bf16[2,2,2,2,96,768]{5,4,3,2,1,0:T(8,128)(2,1)} %dynamic-slice_bitcast_fusion.1), channel_id=1, source_target_pairs={{0,1},{1,0},{2,3},{3,2},{4,5},{5,4},{6,7},{7,6},{8,9},{9,8},{10,11... | collective-permute-start | bytes 7077896 | tf_op jit(solution)/shard_map/ppermute | solution.py:216
  287.6 39.9 %collective-permute-start.15 = (bf16[2,2,2,2,24,3072]{5,4,3,2,1,0:T(8,128)(2,1)}, bf16[2,2,2,2,24,3072]{5,4,3,2,1,0:T(8,128)(2,1)}, u32[]{:S(2)}, u32[]{:S(2)}) collective-permute-start(bf16[2,2,2,2,24,3072]{5,4,3,2,1,0:T(8,128)(2,1)} %dynamic-slice_bitcast_fusion.2), channel_id=1, source_target_pairs={{0,1},{1,0},{2,3},{3,2},{4,5},{5,4},{6,7},{7,6},{8,9},{9,8},{10,11... | collective-permute-start | bytes 7077896 | tf_op jit(solution)/shard_map/ppermute | solution.py:216
  310.8 20.6 %collective-permute-start.10 = (bf16[2,2,2,2,24,3200]{5,4,3,2,1,0:T(8,128)(2,1)}, bf16[2,2,2,2,24,3200]{5,4,3,2,1,0:T(8,128)(2,1)}, u32[]{:S(2)}, u32[]{:S(2)}) collective-permute-start(bf16[2,2,2,2,24,3200]{5,4,3,2,1,0:T(8,128)(2,1)} %dynamic-slice_bitcast_fusion), channel_id=1, source_target_pairs={{0,1},{1,0},{2,3},{3,2},{4,5},{5,4},{6,7},{7,6},{8,9},{9,8},{10,11... | collective-permute-start | bytes 7372808 | tf_op jit(solution)/shard_map/ppermute | solution.py:216
  326.4 16.3 %collective-permute-start.21 = (bf16[2,2,2,96,768]{4,3,0,1,2:T(8,128)(2,1)S(1)}, bf16[2,2,2,96,768]{4,3,0,1,2:T(8,128)(2,1)S(1)}, u32[]{:S(2)}, u32[]{:S(2)}) collective-permute-start(bf16[2,2,2,96,768]{4,3,0,1,2:T(8,128)(2,1)S(1)} %fusion.20), channel_id=1, source_target_pairs={{0,4},{1,3},{2,6},{3,1},{4,0},{5,7},{6,2},{7,5},{8,12},{9,11},{10,... | collective-permute-start | bytes 3538952 | tf_op jit(solution)/shard_map/ppermute | solution.py:216
  330.4 31.3 %collective-permute-start.16 = (bf16[2,2,2,24,3072]{4,3,0,1,2:T(8,128)(2,1)S(1)}, bf16[2,2,2,24,3072]{4,3,0,1,2:T(8,128)(2,1)S(1)}, u32[]{:S(2)}, u32[]{:S(2)}) collective-permute-start(bf16[2,2,2,24,3072]{4,3,0,1,2:T(8,128)(2,1)S(1)} %fusion.22), channel_id=1, source_target_pairs={{0,4},{1,3},{2,6},{3,1},{4,0},{5,7},{6,2},{7,5},{8,12},{9,11},{10,... | collective-permute-start | bytes 3538952 | tf_op jit(solution)/shard_map/ppermute | solution.py:216
  334.1 47.0 %collective-permute-start.11 = (bf16[2,2,2,24,3200]{4,3,2,1,0:T(8,128)(2,1)S(1)}, bf16[2,2,2,24,3200]{4,3,2,1,0:T(8,128)(2,1)S(1)}, u32[]{:S(2)}, u32[]{:S(2)}) collective-permute-start(bf16[2,2,2,24,3200]{4,3,2,1,0:T(8,128)(2,1)S(1)} %fusion.18), channel_id=1, source_target_pairs={{0,4},{1,3},{2,6},{3,1},{4,0},{5,7},{6,2},{7,5},{8,12},{9,11},{10,... | collective-permute-start | bytes 3686408 | tf_op jit(solution)/shard_map/ppermute | solution.py:216
  343.1 40.0 %collective-permute-start.22 = (bf16[2,2,96,768]{3,2,0,1:T(8,128)(2,1)S(1)}, bf16[2,2,96,768]{3,2,0,1:T(8,128)(2,1)S(1)}, u32[]{:S(2)}, u32[]{:S(2)}) collective-permute-start(bf16[2,2,96,768]{3,2,0,1:T(8,128)(2,1)S(1)} %fusion.36), channel_id=1, source_target_pairs={{0,2},{1,5},{2,0},{3,7},{4,6},{5,1},{6,4},{7,3},{8,10},{9,13},{10,... | collective-permute-start | bytes 1769480 | tf_op jit(solution)/shard_map/ppermute | solution.py:216
  362.3 21.0 %collective-permute-start.17 = (bf16[2,2,24,3072]{3,2,0,1:T(8,128)(2,1)S(1)}, bf16[2,2,24,3072]{3,2,0,1:T(8,128)(2,1)S(1)}, u32[]{:S(2)}, u32[]{:S(2)}) collective-permute-start(bf16[2,2,24,3072]{3,2,0,1:T(8,128)(2,1)S(1)} %fusion.35), channel_id=1, source_target_pairs={{0,2},{1,5},{2,0},{3,7},{4,6},{5,1},{6,4},{7,3},{8,10},{9,13},{10,... | collective-permute-start | bytes 1769480 | tf_op jit(solution)/shard_map/ppermute | solution.py:216
  381.5 10.2 %collective-permute-start.12 = (bf16[2,2,24,3200]{3,2,1,0:T(8,128)(2,1)S(1)}, bf16[2,2,24,3200]{3,2,1,0:T(8,128)(2,1)S(1)}, u32[]{:S(2)}, u32[]{:S(2)}) collective-permute-start(bf16[2,2,24,3200]{3,2,1,0:T(8,128)(2,1)S(1)} %fusion.34), channel_id=1, source_target_pairs={{0,2},{1,5},{2,0},{3,7},{4,6},{5,1},{6,4},{7,3},{8,10},{9,13},{10,... | collective-permute-start | bytes 1843208 | tf_op jit(solution)/shard_map/ppermute | solution.py:216
  383.3 17.5 %collective-permute-start.23 = (bf16[2,96,768]{2,1,0:T(8,128)(2,1)S(1)}, bf16[2,96,768]{2,1,0:T(8,128)(2,1)S(1)}, u32[]{:S(2)}, u32[]{:S(2)}) collective-permute-start(bf16[2,96,768]{2,1,0:T(8,128)(2,1)S(1)} %fusion.42), channel_id=1, source_target_pairs={{0,8},{1,9},{2,10},{3,11},{4,12},{5,13},{6,14},{7,15},{8,0},{9,1},... | collective-permute-start | bytes 884744 | tf_op jit(solution)/shard_map/ppermute | solution.py:216
  383.5 16.0 %collective-permute-start.18 = (bf16[2,24,3072]{2,1,0:T(8,128)(2,1)S(1)}, bf16[2,24,3072]{2,1,0:T(8,128)(2,1)S(1)}, u32[]{:S(2)}, u32[]{:S(2)}) collective-permute-start(bf16[2,24,3072]{2,1,0:T(8,128)(2,1)S(1)} %fusion.41), channel_id=1, source_target_pairs={{0,8},{1,9},{2,10},{3,11},{4,12},{5,13},{6,14},{7,15},{8,0},{9,1},... | collective-permute-start | bytes 884744 | tf_op jit(solution)/shard_map/ppermute | solution.py:216
  391.9 21.6 %collective-permute-start.13 = (bf16[2,24,3200]{2,1,0:T(8,128)(2,1)S(1)}, bf16[2,24,3200]{2,1,0:T(8,128)(2,1)S(1)}, u32[]{:S(2)}, u32[]{:S(2)}) collective-permute-start(bf16[2,24,3200]{2,1,0:T(8,128)(2,1)S(1)} %fusion.40), channel_id=1, source_target_pairs={{0,8},{1,9},{2,10},{3,11},{4,12},{5,13},{6,14},{7,15},{8,0},{9,1},... | collective-permute-start | bytes 921608 | tf_op jit(solution)/shard_map/ppermute | solution.py:216
  399.6 13.1 %collective-permute-start.19 = (bf16[24,3072]{1,0:T(8,128)(2,1)S(1)}, bf16[24,3072]{1,0:T(8,128)(2,1)S(1)}, u32[]{:S(2)}, u32[]{:S(2)}) collective-permute-start(bf16[24,3072]{1,0:T(8,128)(2,1)S(1)} %fusion.46), channel_id=1, source_target_pairs={{0,16},{1,17},{2,18},{3,19},{4,20},{5,21},{6,22},{7,23},{8,24},{9,... | collective-permute-start | bytes 442376 | tf_op jit(solution)/shard_map/ppermute | solution.py:216
  400.9 14.8 %collective-permute-start.24 = (bf16[96,768]{1,0:T(8,128)(2,1)S(1)}, bf16[96,768]{1,0:T(8,128)(2,1)S(1)}, u32[]{:S(2)}, u32[]{:S(2)}) collective-permute-start(bf16[96,768]{1,0:T(8,128)(2,1)S(1)} %fusion.47), channel_id=1, source_target_pairs={{0,16},{1,17},{2,18},{3,19},{4,20},{5,21},{6,22},{7,23},{8,24},{9,... | collective-permute-start | bytes 442376 | tf_op jit(solution)/shard_map/ppermute | solution.py:216
  413.5 6.2 %collective-permute-start.14 = (bf16[24,3200]{1,0:T(8,128)(2,1)S(1)}, bf16[24,3200]{1,0:T(8,128)(2,1)S(1)}, u32[]{:S(2)}, u32[]{:S(2)}) collective-permute-start(bf16[24,3200]{1,0:T(8,128)(2,1)S(1)} %fusion.45), channel_id=1, source_target_pairs={{0,16},{1,17},{2,18},{3,19},{4,20},{5,21},{6,22},{7,23},{8,24},{9,... | collective-permute-start | bytes 460808 | tf_op jit(solution)/shard_map/ppermute | solution.py:216
  (44 other events, 426.5 us)
Sparse Core Ops, SparseCore 0:
  11.1 99.5 all-gather.1
